TPU v7x, 32 devices: a whole 2x2x4 slice. The times are simulated.
32 devices in a mesh: rows: 8 (over z, core), cols: 4 (over y, x).
Axes of the slice: x: 2, y: 2, z: 4, core: 2. Of those that a mesh axis runs over, the one named last changes fastest.
Arguments:
- wave_coarse: float32 [192, 192, 192], P('rows', 'cols'), may hold values from -6 to 6
- potential_coarse: float32 [192, 192, 192], P('rows', 'cols'), may hold values from 0 to 5
- potential_fine: float32 [384, 384, 384], P('cols', 'rows'), may hold values from 0 to 5
Outputs:
- fine_wave: float32 [384, 384, 384], P('cols', 'rows')
All inputs are finite; a program needn't handle non-finite values.
Results may differ from a plain program's by a relative error of at most 0.0003.
Values sent between devices are 32-bit elements; how exact they have to be, the bound alone decides.
A program may use at most 128 MiB of HBM per device.

v0:
```python
from functools import partial
import math

import jax
import jax.numpy as jnp
from jax import lax
from jax.sharding import PartitionSpec as P

NC = 192
NF = 384


TIME_STEP = 0.5
CONTACT = 0.4
DIPOLE_STRENGTH = 0.3
EPSILON = 1e-06
HIGHEST = lax.Precision.HIGHEST


def cas_values(product, length):
    phases = 2.0 * math.pi / length * (product % length).astype(jnp.float32)
    return jnp.cos(phases) + jnp.sin(phases)


def cas_matrix(length):
    positions = jnp.arange(length, dtype=jnp.int32)
    return cas_values(positions[:, None] * positions[None, :], length)


def lifted_positions(length):
    positions = jnp.arange(length, dtype=jnp.int32)
    return jnp.where(positions < length // 2, positions, positions + length)


def lift_matrix(length):
    lifted = lifted_positions(length)
    fine_points = jnp.arange(2 * length, dtype=jnp.int32)
    return cas_values(lifted[:, None] * fine_points[None, :], 2 * length)


def wavenumbers(length, block_count, offset, spacing):
    positions = offset + jnp.arange(block_count, dtype=jnp.int32)
    signed = jnp.where(positions < length // 2, positions, positions - length)
    return 2.0 * math.pi / (length * spacing) * signed.astype(jnp.float32)


def multipliers(along_x, along_y, along_z, length):
    squares = along_x + along_y + along_z
    volume = float(length) ** 3
    kinetic = jnp.exp(-0.5 * TIME_STEP * squares) / volume
    nonzero = jnp.where(squares > 0, squares, 1.0)
    dipolar = (
        jnp.where(squares > 0, DIPOLE_STRENGTH * (3.0 * along_z - squares) / nonzero, 0.0) / volume
    )
    return (kinetic, dipolar)


def sweep_out(values, matrix):
    turned = jnp.dot(values, matrix, precision=HIGHEST)
    turned = lax.all_to_all(turned, "cols", split_axis=2, concat_axis=1, tiled=True)
    turned = jnp.einsum("ayc,yk->ack", turned, matrix, precision=HIGHEST)
    turned = lax.all_to_all(turned, "rows", split_axis=2, concat_axis=0, tiled=True)
    return jnp.einsum("xbc,xk->bck", turned, matrix, precision=HIGHEST)


def sweep_back(values, matrix):
    turned = jnp.dot(values, matrix, precision=HIGHEST)
    turned = lax.all_to_all(turned, "rows", split_axis=2, concat_axis=1, tiled=True)
    turned = jnp.einsum("cyb,yk->cbk", turned, matrix, precision=HIGHEST)
    turned = lax.all_to_all(turned, "cols", split_axis=2, concat_axis=0, tiled=True)
    return jnp.einsum("zab,zk->abk", turned, matrix, precision=HIGHEST)


def sweep_lift(values, matrix):
    turned = jnp.einsum("zba,zk->bak", values, matrix, precision=HIGHEST)
    turned = lax.all_to_all(turned, "cols", split_axis=2, concat_axis=0, tiled=True)
    turned = jnp.einsum("yac,yk->ack", turned, matrix, precision=HIGHEST)
    turned = lax.all_to_all(turned, "rows", split_axis=2, concat_axis=0, tiled=True)
    return jnp.einsum("xbc,xk->bck", turned, matrix, precision=HIGHEST)


def advance(evolved, potential, dipolar, volume, forward, inverse):
    density = evolved * evolved
    field_dd = inverse(dipolar * forward(density))
    damped = jnp.exp(-TIME_STEP * (potential + CONTACT * density + field_dd)) * evolved
    squares = lax.psum(jnp.sum(damped * damped), ("rows", "cols"))
    return damped * lax.rsqrt(squares / volume + EPSILON)


def per_device(wave_coarse, potential_coarse, potential_fine):
    row_index = lax.axis_index("rows")
    col_index = lax.axis_index("cols")
    row_count = lax.axis_size("rows")
    col_count = lax.axis_size("cols")
    coarse_matrix = cas_matrix(NC)
    fine_matrix = cas_matrix(NF)
    z_block = NC // col_count
    y_block = NC // row_count
    along_z = wavenumbers(NC, z_block, col_index * z_block, 2.0)[:, None, None] ** 2
    along_y = wavenumbers(NC, y_block, row_index * y_block, 2.0)[None, :, None] ** 2
    along_x = wavenumbers(NC, NC, 0, 2.0)[None, None, :] ** 2
    kinetic, dipolar = multipliers(along_x, along_y, along_z, NC)
    coarse_forward = partial(sweep_out, matrix=coarse_matrix)
    coarse_inverse = partial(sweep_back, matrix=coarse_matrix)
    amplitude = wave_coarse
    evolved = coarse_inverse(kinetic * coarse_forward(amplitude))
    amplitude = advance(
        evolved, potential_coarse, dipolar, float(NC) ** 3, coarse_forward, coarse_inverse
    )
    first_evolved = None
    spectrum = sweep_out(amplitude, coarse_matrix)
    placed = lax.all_to_all(
        lax.all_to_all(spectrum, "rows", split_axis=2, concat_axis=1, tiled=True),
        "cols",
        split_axis=1,
        concat_axis=0,
        tiled=True,
    )
    y_part = NC // col_count
    x_part = NC // row_count
    lift_z = wavenumbers(NC, NC, 0, 2.0)[:, None, None] ** 2
    lift_y = wavenumbers(NC, y_part, col_index * y_part, 2.0)[None, :, None] ** 2
    lift_x = wavenumbers(NC, x_part, row_index * x_part, 2.0)[None, None, :] ** 2
    compact = jnp.exp(-0.5 * TIME_STEP * (lift_x + lift_y + lift_z)) / float(NC) ** 3
    first_evolved = sweep_lift(compact * placed, lift_matrix(NC))
    x_block = NF // row_count
    y_block = NF // col_count
    along_x = wavenumbers(NF, x_block, row_index * x_block, 1.0)[:, None, None] ** 2
    along_y = wavenumbers(NF, y_block, col_index * y_block, 1.0)[None, :, None] ** 2
    along_z = wavenumbers(NF, NF, 0, 1.0)[None, None, :] ** 2
    forward = partial(sweep_back, matrix=fine_matrix)
    inverse = partial(sweep_out, matrix=fine_matrix)
    kinetic, dipolar = multipliers(along_x, along_y, along_z, NF)
    amplitude = advance(first_evolved, potential_fine, dipolar, float(NF) ** 3, forward, inverse)
    return amplitude


def solution(mesh):
    placed = (P("rows", "cols", None), P("rows", "cols", None), P("cols", "rows", None))
    return jax.shard_map(
        per_device, mesh=mesh, in_specs=placed, out_specs=P("cols", "rows", None), check_vma=False
    )
```

profile of v0, /device:TPU:0, one launch (start us, length us, event | category | flops | bytes accessed | tf_op | source)
XLA Modules:
  0.0 1652.1 jit_solution(14188118718066589180)
XLA Ops:
  8.7 18.0 %all_to_all.324 = f32[4,1,55296]{2,1,0:T(1,128)S(1)} all-to-all(f32[4,1,55296]{2,1,0:T(1,128)S(1)} %reshape.219), channel_id=1, replica_groups=mesh['rows'=8,'cols'=4] {'cols'}, dimensions={0} | all-to-all | bytes 1769472 | tf_op jit(solution)/shard_map/all_to_all | solution.py:60
  51.1 22.3 %all-to-all-done.1 = f32[8,1,27648]{2,1,0:T(1,128)S(1)} async-done(((f32[8,1,27648]{2,1,0:T(1,128)}), f32[8,1,27648]{2,1,0:T(1,128)S(1)}, u32[]{:S(2)}, u32[]{:S(2)}) %all-to-all-start.1) | async-done | bytes 884768 | tf_op jit(solution)/shard_map/all_to_all | solution.py:62
  91.1 25.7 %all_to_all.325 = f32[8,1,27648]{2,1,0:T(1,128)S(1)} all-to-all(f32[8,1,27648]{2,1,0:T(1,128)S(1)} %reshape.223), channel_id=1, replica_groups=mesh['rows'=8,'cols'=4] {'rows'}, dimensions={0} | all-to-all | bytes 1769472 | tf_op jit(solution)/shard_map/all_to_all | solution.py:68
  132.2 15.4 all_to_all.326
  202.6 26.7 %all_to_all.328 = f32[8,1,27648]{2,1,0:T(1,128)S(1)} all-to-all(f32[8,1,27648]{2,1,0:T(1,128)} %reshape.229), channel_id=1, replica_groups=mesh['rows'=8,'cols'=4] {'rows'}, dimensions={0} | all-to-all | bytes 1769472 | tf_op jit(solution)/shard_map/all_to_all | solution.py:62
  250.0 26.9 %all_to_all.329 = f32[8,1,27648]{2,1,0:T(1,128)S(1)} all-to-all(f32[8,1,27648]{2,1,0:T(1,128)} %reshape.231), channel_id=1, replica_groups=mesh['rows'=8,'cols'=4] {'rows'}, dimensions={0} | all-to-all | bytes 1769472 | tf_op jit(solution)/shard_map/all_to_all | solution.py:68
  295.4 16.2 all_to_all.330
  328.2 38.1 %psum.14 = f32[]{:T(128)} all-reduce(f32[]{:T(128)} %get-tuple-element.5), channel_id=1, replica_groups=mesh['rows'=8,'cols'=4] {'rows','cols'}, use_global_device_ids=true, to_apply=%region_1.2 | all-reduce | flops 1 | bytes 8 | tf_op jit(solution)/shard_map/psum | solution.py:86
  372.4 15.6 all_to_all.331
  405.2 26.2 %all_to_all.332 = f32[8,1,27648]{2,1,0:T(1,128)S(1)} all-to-all(f32[8,1,27648]{2,1,0:T(1,128)S(1)} %reshape.237), channel_id=1, replica_groups=mesh['rows'=8,'cols'=4] {'rows'}, dimensions={0} | all-to-all | bytes 1769472 | tf_op jit(solution)/shard_map/all_to_all | solution.py:62
  446.8 25.4 %all_to_all.333 = f32[8,1,27648]{2,1,0:T(1,128)S(1)} all-to-all(f32[8,1,27648]{2,1,0:T(1,128)S(1)} %reshape.239), channel_id=1, replica_groups=mesh['rows'=8,'cols'=4] {'rows'}, dimensions={0} | all-to-all | bytes 1769472 | tf_op jit(solution)/shard_map/all_to_all | solution.py:113
  522.6 25.2 %all_to_all.334 = f32[4,1,110592]{2,1,0:T(1,128)} all-to-all(f32[4,1,110592]{2,1,0:T(1,128)S(1)} %reshape.243), channel_id=1, replica_groups=mesh['rows'=8,'cols'=4] {'cols'}, dimensions={0} | all-to-all | bytes 3538944 | tf_op jit(solution)/shard_map/all_to_all | solution.py:76
  578.4 109.0 %all_to_all.335 = f32[24,96,384]{1,0,2:T(8,128)S(1)} all-to-all(f32[24,96,384]{1,0,2:T(8,128)} %copy.235), channel_id=1, replica_groups=mesh['rows'=8,'cols'=4] {'rows'}, dimensions={2} | all-to-all | bytes 7077888 | tf_op jit(solution)/shard_map/all_to_all | solution.py:78
  713.2 20.2 %fusion.8 = f32[96,48,384]{2,1,0:T(8,128)} fusion(f32[96,48,384]{2,1,0:T(8,128)S(1)} %fusion.57), kind=kOutput, calls=%fused_computation.13 | convolution fusion | flops 8156971008 | bytes 14155776 | tf_op jit(solution)/shard_map/dot_general | solution.py:67
  742.5 210.2 %all_to_all.336 = f32[96,48,384]{0,1,2:T(8,128)S(1)} all-to-all(f32[96,48,384]{0,1,2:T(8,128)} %copy.239), channel_id=1, replica_groups=mesh['rows'=8,'cols'=4] {'rows'}, dimensions={2} | all-to-all | bytes 14155776 | tf_op jit(solution)/shard_map/all_to_all | solution.py:68
  968.2 21.9 %fusion.44 = f32[96,48,384]{2,1,0:T(8,128)} fusion(f32[96,384,48]{1,2,0:T(8,128)} %copy.242), kind=kOutput, calls=%fused_computation.66 | convolution fusion | flops 8155201536 | bytes 14155776 | tf_op jit(solution)/shard_map/cyb,yk->cbk/dot_general | solution.py:69
  1005.3 103.4 %all-to-all-done.15 = f32[96,48,384]{0,1,2:T(8,128)} async-done(((f32[96,48,384]{0,1,2:T(8,128)}), f32[96,48,384]{0,1,2:T(8,128)}, u32[]{:S(2)}, u32[]{:S(2)}) %all-to-all-start.15) | async-done | bytes 7077920 | tf_op jit(solution)/shard_map/all_to_all | solution.py:70
  1132.5 21.2 %fusion.42 = f32[48,96,384]{2,1,0:T(8,128)S(1)} fusion(f32[384,48,96]{0,2,1:T(8,128)} %all_to_all.297), kind=kOutput, calls=%fused_computation.64 | convolution fusion | flops 8155201536 | bytes 14155776 | tf_op jit(solution)/shard_map/zab,zk->abk/dot_general | solution.py:71
  1153.7 20.4 %fusion.3 = f32[48,96,384]{2,1,0:T(8,128)} fusion(f32[48,96,384]{2,1,0:T(8,128)S(1)} %fusion.42, f32[384]{0:T(512)S(1)} %get-tuple-element.12, f32[384]{0:T(512)S(1)} %get-tuple-element.11, f32[48,96]{1,0:T(8,128)S(1)} %broadcast_add_fusion), kind=kOutput, calls=%fused_computation.8 | convolution fusion | flops 8171126784 | bytes 14177280 | tf_op jit(solution)/shard_map/dot_general | solution.py:59
  1183.1 111.9 %all_to_all.337 = f32[48,96,384]{1,0,2:T(8,128)} all-to-all(f32[48,96,384]{1,0,2:T(8,128)} %copy.245), channel_id=1, replica_groups=mesh['rows'=8,'cols'=4] {'cols'}, dimensions={2} | all-to-all | bytes 14155776 | tf_op jit(solution)/shard_map/all_to_all | solution.py:60
  1318.8 21.9 %fusion.39 = f32[48,96,384]{2,1,0:T(8,128)} fusion(f32[48,384,96]{1,2,0:T(8,128)} %all_to_all.301), kind=kOutput, calls=%fused_computation.61 | convolution fusion | flops 8155201536 | bytes 14155776 | tf_op jit(solution)/shard_map/ayc,yk->ack/dot_general | solution.py:61
  1349.7 210.4 %all_to_all.338 = f32[48,96,384]{1,0,2:T(8,128)S(1)} all-to-all(f32[48,96,384]{1,0,2:T(8,128)} %copy.247), channel_id=1, replica_groups=mesh['rows'=8,'cols'=4] {'rows'}, dimensions={2} | all-to-all | bytes 14155776 | tf_op jit(solution)/shard_map/all_to_all | solution.py:62
  1575.6 31.6 %multiply_reduce_fusion = (f32[]{:T(128)}, f32[96,48,384]{2,1,0:T(8,128)}) fusion(f32[96,48,384]{2,1,0:T(8,128)} %copy-done.2, f32[384,96,48]{0,2,1:T(8,128)} %copy.250, f32[96,48,384]{2,1,0:T(8,128)} %param.5), kind=kOutput, calls=%fused_computation.11 | convolution fusion | flops 8169357312 | bytes 28311556 | tf_op jit(solution)/shard_map/xbc,xk->bck/dot_general | solution.py:63
  1607.1 37.6 %psum.15 = f32[]{:T(128)} all-reduce(f32[]{:T(128)} %get-tuple-element.7), channel_id=1, replica_groups=mesh['rows'=8,'cols'=4] {'rows','cols'}, use_global_device_ids=true, to_apply=%region_3.4 | all-reduce | flops 1 | bytes 8 | tf_op jit(solution)/shard_map/psum | solution.py:86
  (138 shorter events, 448.5 us)
Async XLA Ops:
  0.0 1.3 copy-start
  45.3 28.1 %all-to-all-start.1 = ((f32[8,1,27648]{2,1,0:T(1,128)}), f32[8,1,27648]{2,1,0:T(1,128)S(1)}, u32[]{:S(2)}, u32[]{:S(2)}) async-start(f32[8,1,27648]{2,1,0:T(1,128)} %reshape.221), calls=%async_computation.1 | async-start | bytes 1769472 | tf_op jit(solution)/shard_map/all_to_all | solution.py:62
  81.2 2.4 copy-start.4
  237.2 2.4 copy-start.5
  482.5 15.7 all-to-all-start.11
  507.5 2.5 copy-start.3
  710.2 3.0 copy-start.2
  999.2 109.5 %all-to-all-start.15 = ((f32[96,48,384]{0,1,2:T(8,128)}), f32[96,48,384]{0,1,2:T(8,128)}, u32[]{:S(2)}, u32[]{:S(2)}) async-start(f32[96,48,384]{0,1,2:T(8,128)} %copy.243), calls=%async_computation.15 | async-start | bytes 18874368 | tf_op jit(solution)/shard_map/all_to_all | solution.py:70
  1645.4 6.5 copy-start.1
where the time goes:
time: 1660 us; the launch traced here: 1650 us
  blocking collectives  954 us (57%)
  local copies, waits for them, and re-layouts  287 us (17%)
  matrix products  202 us (12%)
  waiting for transfers between devices  137 us (8%)
  other arithmetic  56.5 us (3%)
    all_to_all x3, blocking collectives, sweep_out(): lax.all_to_all(turned, 'rows', split_axis=2, concat_axis=0, tiled=True)  263 us
    all_to_all x3, blocking collectives, sweep_back(): lax.all_to_all(turned, 'rows', split_axis=2, concat_axis=1, tiled=True)  263 us
    all_to_all x4, blocking collectives, sweep_out(): lax.all_to_all(turned, 'cols', split_axis=2, concat_axis=1, tiled=True)  161 us
    all_to_all x1, blocking collectives, sweep_lift(): lax.all_to_all(turned, 'rows', split_axis=2, concat_axis=0, tiled=True)  109 us
    all_to_all x1, waiting for transfers between devices, sweep_back(): lax.all_to_all(turned, 'cols', split_axis=2, concat_axis=0, tiled=True)  103 us
    psum x2, blocking collectives, advance(): squares = lax.psum(jnp.sum(damped * damped), ('rows', 'cols'))  75.8 us
    unnamed x38, local copies, waits for them, and re-layouts  68.3 us
    all_to_all x9, local copies, waits for them, and re-layouts, sweep_out(): lax.all_to_all(turned, 'cols', split_axis=2, concat_axis=1, tiled=True)  40.4 us
  transfers between devices with their start and end apart: 3, of which 3 were waited for; matrix products, arithmetic and copies ran while one was open for 0% of the time, Pallas kernels for 0%

commit v1 on v0

v1 whole, which is shorter than its diff:
```python
import functools
import math

import jax
import jax.numpy as jnp
from jax import lax
from jax.experimental import pallas as pl
from jax.experimental.pallas import tpu as pltpu
from jax.sharding import PartitionSpec as P

TIME_STEP = 0.5
CONTACT = 0.4
DIPOLE_STRENGTH = 0.3
EPSILON = 1e-06
HIGH = lax.Precision.HIGH
HIGHEST = lax.Precision.HIGHEST
MESH = pl.DeviceIdType.MESH


def cas_values(product, length):
    phases = 2.0 * math.pi / length * (product % length).astype(jnp.float32)
    return jnp.cos(phases) + jnp.sin(phases)


def cas_matrix(length):
    positions = jnp.arange(length, dtype=jnp.int32)
    return cas_values(positions[:, None] * positions[None, :], length)


def lift_matrix(length):
    positions = jnp.arange(length, dtype=jnp.int32)
    lifted = jnp.where(positions < length // 2, positions, positions + length)
    fine_points = jnp.arange(2 * length, dtype=jnp.int32)
    return cas_values(lifted[:, None] * fine_points[None, :], 2 * length)


def wavenumbers(length, block_count, offset, spacing):
    positions = offset + jnp.arange(block_count, dtype=jnp.int32)
    signed = jnp.where(positions < length // 2, positions, positions - length)
    return 2.0 * math.pi / (length * spacing) * signed.astype(jnp.float32)


def dipolar_weights(along_x, along_y, along_z, length):
    squares = along_x + along_y + along_z
    nonzero = jnp.where(squares > 0, squares, 1.0)
    weights = jnp.where(squares > 0, DIPOLE_STRENGTH * (3.0 * along_z - squares) / nonzero, 0.0)
    return weights / float(length) ** 3


def exchange_kernel(axes, sizes, *refs):
    count = len(axes)
    sources, targets = refs[:count], refs[count : 2 * count]
    send_sems, recv_sems, local_sems = refs[2 * count :]
    row, col = lax.axis_index("rows"), lax.axis_index("cols")

    def place(axis, index):
        return (index, col) if axis == "rows" else (row, index)

    barrier = pltpu.get_barrier_semaphore()
    waits = 0
    for axis in sorted(set(axes)):
        size = sizes[axis]
        me = lax.axis_index(axis)
        for step in range(1, size):
            peer = lax.rem(me + step, size)
            pl.semaphore_signal(barrier, inc=1, device_id=place(axis, peer), device_id_type=MESH)
        waits += size - 1
    pl.semaphore_wait(barrier, waits)
    most = max(sizes[axis] for axis in axes)
    order = sorted(range(1, most), key=lambda step: abs(2 * step - most))
    copies = []
    for step in order:
        for index, axis in enumerate(axes):
            size = sizes[axis]
            if step >= size:
                continue
            me = lax.axis_index(axis)
            peer = lax.rem(me + step, size)
            copy = pltpu.make_async_remote_copy(
                src_ref=sources[index].at[peer],
                dst_ref=targets[index].at[me],
                send_sem=send_sems.at[index, step],
                recv_sem=recv_sems.at[index, step],
                device_id=place(axis, peer),
                device_id_type=MESH,
            )
            copy.start()
            copies.append(copy)
    for index, axis in enumerate(axes):
        me = lax.axis_index(axis)
        copy = pltpu.make_async_copy(
            sources[index].at[me], targets[index].at[me], local_sems.at[index]
        )
        copy.start()
        copies.append(copy)
    for copy in copies:
        copy.wait()


class Exchanger:
    def __init__(self, sizes):
        self.sizes = sizes
        self.calls = 0

    def __call__(self, *pairs):
        arrays = [array for array, _ in pairs]
        axes = tuple(axis for _, axis in pairs)
        most = max(self.sizes.values())
        count = len(arrays)
        self.calls += 1
        return pl.pallas_call(
            functools.partial(exchange_kernel, axes, self.sizes),
            out_shape=[jax.ShapeDtypeStruct(a.shape, a.dtype) for a in arrays],
            in_specs=[pl.BlockSpec(memory_space=pl.ANY)] * count,
            out_specs=[pl.BlockSpec(memory_space=pl.ANY)] * count,
            scratch_shapes=[
                pltpu.SemaphoreType.DMA((count, most)),
                pltpu.SemaphoreType.DMA((count, most)),
                pltpu.SemaphoreType.DMA((count,)),
            ],
            compiler_params=pltpu.CompilerParams(
                collective_id=self.calls - 1, has_side_effects=True
            ),
            name=f"exchange_{self.calls - 1}",
        )(*arrays)


def give(values, matrix, parts, precision=HIGH):
    if matrix is None:
        turned = jnp.transpose(values, (2, 0, 1))
    else:
        turned = jnp.einsum("abl,lk->kab", values, matrix, precision=precision)
    length, rows_extent, cols_extent = turned.shape
    return turned.reshape(parts, length // parts, rows_extent * cols_extent)


def take(received, axis, rows_extent):
    parts, block, area = received.shape
    cols_extent = area // rows_extent
    received = received.reshape(parts, block, rows_extent, cols_extent)
    if axis == "cols":
        return received.transpose(2, 1, 0, 3).reshape(rows_extent, block, parts * cols_extent)
    return received.transpose(1, 3, 0, 2).reshape(block, cols_extent, parts * rows_extent)


def apply(values, matrix, precision=HIGH):
    return jnp.einsum("abl,lk->abk", values, matrix, precision=precision)


def per_device(sizes, wave_coarse, potential_coarse, potential_fine):
    row, col = lax.axis_index("rows"), lax.axis_index("cols")
    rows, cols = sizes["rows"], sizes["cols"]
    nc, nf = wave_coarse.shape[2], potential_fine.shape[2]
    exchange = Exchanger(sizes)

    coarse_matrix = cas_matrix(nc)
    fine_matrix = cas_matrix(nf)
    decay = jnp.exp(-0.5 * TIME_STEP * wavenumbers(nc, nc, 0, 2.0) ** 2)[:, None] / nc
    evolve = jnp.dot(coarse_matrix, decay * coarse_matrix, precision=HIGHEST)
    lift = jnp.dot(coarse_matrix, decay * lift_matrix(nc), precision=HIGHEST)

    xr, yr, zr = nc // rows, nc // rows, nc // rows
    (got,) = exchange((give(wave_coarse, evolve, cols), "cols"))
    held = take(got, "cols", xr)
    (got,) = exchange((give(held, evolve, rows), "rows"))
    evolved = apply(take(got, "rows", xr), evolve)
    got, back = exchange(
        (give(evolved * evolved, coarse_matrix, cols), "cols"), (give(evolved, None, rows), "rows")
    )
    held, back = take(got, "cols", yr), take(back, "rows", yr)
    got, back = exchange(
        (give(held, coarse_matrix, rows), "rows"), (give(back, None, cols), "cols")
    )
    spectrum, evolved = take(got, "rows", yr), take(back, "cols", xr)
    z_block, x_block = nc // rows, nc // cols
    weights = dipolar_weights(
        wavenumbers(nc, x_block, col * x_block, 2.0)[None, :, None] ** 2,
        wavenumbers(nc, nc, 0, 2.0)[None, None, :] ** 2,
        wavenumbers(nc, z_block, row * z_block, 2.0)[:, None, None] ** 2,
        nc,
    )
    spectrum = weights * apply(spectrum, coarse_matrix)
    (got,) = exchange((give(spectrum, coarse_matrix, cols), "cols"))
    (got,) = exchange((give(take(got, "cols", zr), coarse_matrix, rows), "rows"))
    field_dd = apply(take(got, "rows", zr), coarse_matrix)
    density = evolved * evolved
    damped = jnp.exp(-TIME_STEP * (potential_coarse + CONTACT * density + field_dd)) * evolved
    partial_sum = jnp.sum(damped * damped)

    got, sums = exchange(
        (give(damped, lift, cols), "cols"),
        (jnp.full((cols, 8, 128), partial_sum, jnp.float32), "cols"),
    )
    partial_sum = jnp.sum(sums[:, 0, 0])
    got, sums = exchange(
        (give(take(got, "cols", xr), lift, rows), "rows"),
        (jnp.full((rows, 8, 128), partial_sum, jnp.float32), "rows"),
    )
    scale = lax.rsqrt(jnp.sum(sums[:, 0, 0]) / float(nc) ** 3 + EPSILON)
    evolved = jnp.einsum("abl,lk->bak", take(got, "rows", xr), lift, precision=HIGH) * scale

    density = evolved * evolved
    near, far = fine_matrix[:, : nf // 2], fine_matrix[:, nf // 2 :]
    swapped = density.transpose(1, 0, 2)
    yr = nf // rows
    got_near, got_far = exchange(
        (give(swapped, near, rows), "rows"), (give(swapped, far, cols), "cols")
    )
    near_field, far_field = take(got_near, "rows", yr), take(got_far, "cols", yr)
    near_rows = near_field.shape[0]
    got_near, got_far = exchange(
        (give(near_field, fine_matrix, cols), "cols"), (give(far_field, fine_matrix, rows), "rows")
    )
    near_field = apply(take(got_near, "cols", near_rows), fine_matrix)
    far_field = apply(take(got_far, "rows", yr), fine_matrix)
    y_block, z_block = nf // cols, nf // rows
    near_cols = nf // 2 // rows
    far_cols = nf // 2 // cols
    every = wavenumbers(nf, nf, 0, 1.0)[None, None, :] ** 2
    near_field = near_field * dipolar_weights(
        wavenumbers(nf, near_cols, row * near_cols, 1.0)[:, None, None] ** 2,
        wavenumbers(nf, y_block, col * y_block, 1.0)[None, :, None] ** 2,
        every,
        nf,
    )
    far_field = far_field * dipolar_weights(
        wavenumbers(nf, far_cols, nf // 2 + col * far_cols, 1.0)[None, :, None] ** 2,
        every,
        wavenumbers(nf, z_block, row * z_block, 1.0)[:, None, None] ** 2,
        nf,
    )
    got_near, got_far = exchange(
        (give(near_field, fine_matrix, cols), "cols"), (give(far_field, fine_matrix, rows), "rows")
    )
    near_field, far_field = take(got_near, "cols", near_rows), take(got_far, "rows", z_block)
    got_near, got_far = exchange(
        (give(near_field, fine_matrix, rows), "rows"), (give(far_field, fine_matrix, cols), "cols")
    )
    near_field, far_field = take(got_near, "rows", near_rows), take(got_far, "cols", yr)
    spectrum = jnp.concatenate([near_field, far_field], axis=2)
    field_dd = jnp.einsum("abl,lk->bak", spectrum, fine_matrix, precision=HIGH)
    damped = jnp.exp(-TIME_STEP * (potential_fine + CONTACT * density + field_dd)) * evolved
    total = jnp.sum(damped * damped)
    for axis in ("rows", "cols"):
        (sums,) = exchange((jnp.full((sizes[axis], 8, 128), total, jnp.float32), axis))
        total = jnp.sum(sums[:, 0, 0])
    return damped * lax.rsqrt(total / float(nf) ** 3 + EPSILON)


def solution(mesh):
    sizes = {"rows": mesh.shape["rows"], "cols": mesh.shape["cols"]}
    placed = (P("rows", "cols", None), P("rows", "cols", None), P("cols", "rows", None))
    return jax.shard_map(
        functools.partial(per_device, sizes),
        mesh=mesh,
        in_specs=placed,
        out_specs=P("cols", "rows", None),
        check_vma=False,
    )
```

time: 1660 us -> 1040 us (0.63)
  blocking collectives: 954 us -> 0 us
  Pallas kernels: 0 us -> 550 us
  waiting for transfers between devices: 137 us -> 0 us
  matrix products: 202 us -> 145 us
  other arithmetic: 56.5 us -> 17.5 us
  local copies, waits for them, and re-layouts: 287 us -> 314 us
    all_to_all x15 -> x0, blocking collectives: 878 us -> none  [the longest x3 263 us: sweep_out(): lax.all_to_all(turned, 'rows', split_axis=2, concat_axis=0, tiled=True)]
    pallas_call x0 -> x14, Pallas kernels: none -> 550 us  [__call__(): pl.pallas_call(functools.partial(exchange_kernel, axes, self.sizes), out_...]
    reshape x0 -> x45, local copies, waits for them, and re-layouts: none -> 201 us  [the longest x24 109 us: take(): received = received.reshape(parts, block, rows_extent, cols_extent)]
    all_to_all x36 -> x0, local copies, waits for them, and re-layouts: 151 us -> none  [the longest x9 40.4 us: sweep_out(): lax.all_to_all(turned, 'cols', split_axis=2, concat_axis=1, tiled=True)]
    all_to_all x3 -> x0, waiting for transfers between devices: 137 us -> none  [the longest x1 103 us: sweep_back(): lax.all_to_all(turned, 'cols', split_axis=2, concat_axis=0, tiled=True)]
    psum x2 -> x0, blocking collectives: 75.8 us -> none  [advance(): squares = lax.psum(jnp.sum(damped * damped), ('rows', 'cols'))]
    unnamed x38 -> x20, local copies, waits for them, and re-layouts: 68.3 us -> 2.05 us
    dot_general x24 -> x25, matrix products: 202 us -> 145 us  [the longest x16 77.6 us: give(): turned = jnp.einsum('abl,lk->kab', values, matrix, precision=precision)]
  transfers between devices with their start and end apart: 3 -> 0, of which waited for: 3 -> 0; matrix products, arithmetic and copies ran while one was open for 0% -> 0% of each run, Pallas kernels for 0% -> 0%
where the time goes in v1:
time: 1040 us; the launch traced here: 1030 us
  Pallas kernels  550 us (53%)
  local copies, waits for them, and re-layouts  314 us (30%)
  matrix products  145 us (14%)
  other arithmetic  17.5 us (2%)
    pallas_call x14, Pallas kernels, __call__(): pl.pallas_call(functools.partial(exchange_kernel, axes, self.sizes), out_...  550 us
    reshape x24, local copies, waits for them, and re-layouts, take(): received = received.reshape(parts, block, rows_extent, cols_extent)  109 us
    dot_general x16, matrix products, give(): turned = jnp.einsum('abl,lk->kab', values, matrix, precision=precision)  77.6 us
    reshape x16, local copies, waits for them, and re-layouts, give(): return turned.reshape(parts, length // parts, rows_extent * cols_extent)  61.7 us
    dot_general x11, local copies, waits for them, and re-layouts, give(): turned = jnp.einsum('abl,lk->kab', values, matrix, precision=precision)  44.7 us
    dot_general x5, matrix products, apply(): return jnp.einsum('abl,lk->abk', values, matrix, precision=precision)  33.6 us
    transpose x8, local copies, waits for them, and re-layouts, take(): received.transpose(2, 1, 0, 3)  33 us
    dot_general x1, matrix products, per_device(): field_dd = jnp.einsum('abl,lk->bak', spectrum, fine_matrix, precision=HIGH)  23.3 us

profile of v1, /device:TPU:0, one launch (start us, length us, event | category | flops | bytes accessed | tf_op | source)
XLA Modules:
  0.0 1029.1 jit_solution(15296155188556676471)
XLA Ops:
  8.2 14.9 %exchange_0.1 = f32[4,48,1152]{2,1,0:T(8,128)} custom-call(f32[4,48,1152]{2,1,0:T(8,128)} %copy.145.refs_0_), custom_call_target="tpu_custom_call" | custom-call | tf_op jit(solution)/shard_map/exchange_0/pallas_call | solution.py:111
  30.9 19.7 %exchange_1.1 = f32[8,24,1152]{2,1,0:T(8,128)} custom-call(f32[8,24,1152]{2,1,0:T(8,128)} %fusion.195.refs_0_), custom_call_target="tpu_custom_call" | custom-call | tf_op jit(solution)/shard_map/exchange_1/pallas_call | solution.py:111
  65.7 23.1 %exchange_2.1 = (f32[4,48,1152]{2,1,0:T(8,128)}, f32[8,24,1152]{2,1,0:T(8,128)}) custom-call(f32[4,48,1152]{2,1,0:T(8,128)} %copy.147.refs_0_, f32[8,24,1152]{2,1,0:T(8,128)} %reshape.505.refs_1_), custom_call_target="tpu_custom_call" | custom-call | tf_op jit(solution)/shard_map/exchange_2/pallas_call | solution.py:111
  104.9 22.7 %exchange_3.1 = (f32[8,24,1152]{2,1,0:T(8,128)}, f32[4,48,1152]{2,1,0:T(8,128)}) custom-call(f32[8,24,1152]{2,1,0:T(8,128)} %fusion.196.refs_0_, f32[4,48,1152]{2,1,0:T(8,128)} %reshape.509.refs_1_), custom_call_target="tpu_custom_call" | custom-call | tf_op jit(solution)/shard_map/exchange_3/pallas_call | solution.py:111
  141.1 13.8 %exchange_4.1 = f32[4,48,1152]{2,1,0:T(8,128)} custom-call(f32[4,48,1152]{2,1,0:T(8,128)} %copy.148.refs_0_), custom_call_target="tpu_custom_call" | custom-call | tf_op jit(solution)/shard_map/exchange_4/pallas_call | solution.py:111
  162.8 21.6 %exchange_5.1 = f32[8,24,1152]{2,1,0:T(8,128)} custom-call(f32[8,24,1152]{2,1,0:T(8,128)} %fusion.197.refs_0_), custom_call_target="tpu_custom_call" | custom-call | tf_op jit(solution)/shard_map/exchange_5/pallas_call | solution.py:111
  218.2 23.4 %exchange_6.1 = (f32[4,96,1152]{2,1,0:T(8,128)}, f32[4,8,128]{2,1,0:T(8,128)}) custom-call(f32[4,96,1152]{2,1,0:T(8,128)} %copy.102.refs_0_, f32[4,8,128]{2,1,0:T(8,128)} %broadcast_in_dim.24.refs_1_), custom_call_target="tpu_custom_call" | custom-call | tf_op jit(solution)/shard_map/exchange_6/pallas_call | solution.py:111
  254.3 64.7 %exchange_7.1 = (f32[8,48,2304]{2,1,0:T(8,128)}, f32[8,8,128]{2,1,0:T(8,128)}) custom-call(f32[8,48,2304]{2,1,0:T(8,128)} %fusion.198.refs_0_, f32[8,8,128]{2,1,0:T(8,128)} %broadcast_in_dim.44.refs_1_), custom_call_target="tpu_custom_call" | custom-call | tf_op jit(solution)/shard_map/exchange_7/pallas_call | solution.py:111
  375.4 79.1 %exchange_8.1 = (f32[8,24,4608]{2,1,0:T(8,128)}, f32[4,48,4608]{2,1,0:T(8,128)}) custom-call(f32[8,24,4608]{2,1,0:T(8,128)} %reshape.522.refs_0_, f32[4,48,4608]{2,1,0:T(8,128)} %reshape.523.refs_1_), custom_call_target="tpu_custom_call" | custom-call | tf_op jit(solution)/shard_map/exchange_8/pallas_call | solution.py:111
  509.7 79.6 %exchange_9.1 = (f32[4,96,2304]{2,1,0:T(8,128)}, f32[8,48,2304]{2,1,0:T(8,128)}) custom-call(f32[4,96,2304]{2,1,0:T(8,128)} %fusion.33.refs_0_, f32[8,48,2304]{2,1,0:T(8,128)} %fusion.199.refs_1_), custom_call_target="tpu_custom_call" | custom-call | tf_op jit(solution)/shard_map/exchange_9/pallas_call | solution.py:111
  589.3 9.5 reshape.529
  598.8 9.6 copy.119
  608.4 8.3 reshape.530
  616.7 10.2 fusion.68
  627.0 10.1 fusion.21
  673.0 10.2 fusion.71
  683.3 10.1 fusion.25
  705.7 79.5 %exchange_10.1 = (f32[4,96,2304]{2,1,0:T(8,128)}, f32[8,48,2304]{2,1,0:T(8,128)}) custom-call(f32[4,96,2304]{2,1,0:T(8,128)} %copy.153.refs_0_, f32[8,48,2304]{2,1,0:T(8,128)} %copy.156.refs_1_), custom_call_target="tpu_custom_call" | custom-call | tf_op jit(solution)/shard_map/exchange_10/pallas_call | solution.py:111
  785.2 9.5 reshape.533
  794.7 9.6 copy.124
  804.3 8.5 reshape.555
  846.0 79.5 %exchange_11.1 = (f32[8,48,2304]{2,1,0:T(8,128)}, f32[4,96,2304]{2,1,0:T(8,128)}) custom-call(f32[8,48,2304]{2,1,0:T(8,128)} %fusion.200.refs_0_, f32[4,96,2304]{2,1,0:T(8,128)} %fusion.201.refs_1_), custom_call_target="tpu_custom_call" | custom-call | tf_op jit(solution)/shard_map/exchange_11/pallas_call | solution.py:111
  960.3 23.3 %multiply_reduce_fusion = (f32[]{:T(128)}, f32[96,48,384]{2,0,1:T(8,128)}) fusion(f32[48,96,192]{2,1,0:T(8,128)} %copy.129, f32[48,96,192]{2,1,0:T(8,128)} %copy.128, f32[384,48,96]{0,2,1:T(8,128)} %fusion.88, f32[]{:T(128)S(6)} %rsqrt.6, f32[96,48,384]{2,1,0:T(8,128)} %param.5), kind=kOutput, calls=%fused_computation.15 | convolution fusion | flops 4096032768 | bytes 28311560 | tf_op jit(solution)/shard_map/abl,lk->bak/dot_general | solution.py:241
  984.8 23.8 %exchange_12.1 = f32[8,8,128]{2,1,0:T(8,128)} custom-call(f32[8,8,128]{2,1,0:T(8,128)} %broadcast_in_dim.47.refs_0_), custom_call_target="tpu_custom_call" | custom-call | tf_op jit(solution)/shard_map/exchange_12/pallas_call | solution.py:111
  (139 shorter events, 362.8 us)
Async XLA Ops:
  0.0 2.0 copy-start
  1.4 0.7 copy-start.4
  25.2 4.2 copy-start.5
  52.8 0.9 copy-start.6
  96.5 5.5 copy-start.7
  157.1 4.2 copy-start.8
  184.4 5.4 copy-start.9
  209.0 0.7 copy-start.2
  243.9 4.2 copy-start.3
  1018.2 10.7 %copy-start.1 = (f32[24,48,192]{2,1,0:T(8,128)S(1)}, f32[24,48,192]{2,1,0:T(8,128)}, u32[]{:S(2)}) copy-start(f32[24,48,192]{2,1,0:T(8,128)} %param.3) | copy-start | bytes 2654212

commit v2 on v1

--- a/solution.py
+++ b/solution.py
@@ -147,6 +147,110 @@
     return jnp.einsum("abl,lk->abk", values, matrix, precision=precision)
 
 
+def split_product(values, matrix):
+    high = matrix.astype(jnp.bfloat16)
+    low = (matrix - high.astype(jnp.float32)).astype(jnp.bfloat16)
+    top = values.astype(jnp.bfloat16)
+    rest = (values - top.astype(jnp.float32)).astype(jnp.bfloat16)
+    product = functools.partial(jnp.dot, preferred_element_type=jnp.float32)
+    return product(top, high) + (product(top, low) + product(rest, high))
+
+
+def gather_pieces(received, held):
+    parts, chunk = received.shape[0], held.shape[0]
+    width = received.shape[2] // chunk
+    for s in range(chunk):
+        for p in range(parts):
+            held[s, :, p * width : (p + 1) * width] = received[p, :, s * width : (s + 1) * width]
+
+
+def scatter_pieces(held, sent):
+    parts, chunk = sent.shape[0], held.shape[0]
+    width = sent.shape[2] // chunk
+    for s in range(chunk):
+        for p in range(parts):
+            sent[p, :, s * width : (s + 1) * width] = held[s, :, p * width : (p + 1) * width]
+
+
+def assemble_kernel(received, matrix, out, held):
+    gather_pieces(received, held)
+    chunk, k, length = held.shape
+    product = split_product(held[...].reshape(chunk * k, length), matrix[...])
+    out[...] = product.reshape(out.shape)
+
+
+def middle_kernel(vertical, volume, received, matrix, sq_s, sq_k, sq_l, sent, held):
+    gather_pieces(received, held)
+    chunk, k, length = held.shape
+    values = split_product(held[...].reshape(chunk * k, length), matrix[...])
+    parts = [sq_s[...], sq_k[...][None], sq_l[...][None]]
+    parts = [jnp.broadcast_to(part, held.shape) for part in parts]
+    squares = parts[0] + parts[1] + parts[2]
+    nonzero = jnp.where(squares > 0, squares, 1.0)
+    weights = jnp.where(
+        squares > 0, DIPOLE_STRENGTH * (3.0 * parts[vertical] - squares) / nonzero, 0.0
+    )
+    values = values * (weights / volume).reshape(chunk * k, length)
+    held[...] = split_product(values, matrix[...]).reshape(held.shape)
+    scatter_pieces(held, sent)
+
+
+def chunk_of(spectators, width, k):
+    for chunk in range(1, spectators):
+        if spectators % chunk == 0 and chunk * width % 128 == 0 and chunk * k >= 256:
+            return chunk
+    return spectators
+
+
+def assemble(received, spectators, matrix):
+    parts, k, area = received.shape
+    chunk = chunk_of(spectators, area // spectators, k)
+    length, points = matrix.shape
+    return pl.pallas_call(
+        assemble_kernel,
+        grid=(spectators // chunk,),
+        in_specs=[
+            pl.BlockSpec((parts, k, area // spectators * chunk), lambda i: (0, 0, i)),
+            pl.BlockSpec((length, points), lambda i: (0, 0)),
+        ],
+        out_specs=pl.BlockSpec((chunk, k, points), lambda i: (i, 0, 0)),
+        out_shape=jax.ShapeDtypeStruct((spectators, k, points), jnp.float32),
+        scratch_shapes=[pltpu.VMEM((chunk, k, length), jnp.float32)],
+    )(received, matrix)
+
+
+def middle(received, matrix, sq_s, sq_k, sq_l, vertical):
+    parts, k, area = received.shape
+    spectators, length = sq_s.shape[0], matrix.shape[0]
+    chunk = chunk_of(spectators, area // spectators, k)
+    block = pl.BlockSpec((parts, k, area // spectators * chunk), lambda i: (0, 0, i))
+    return pl.pallas_call(
+        functools.partial(middle_kernel, vertical, float(length) ** 3),
+        grid=(spectators // chunk,),
+        in_specs=[
+            block,
+            pl.BlockSpec((length, length), lambda i: (0, 0)),
+            pl.BlockSpec((chunk, 1, 1), lambda i: (i, 0, 0)),
+            pl.BlockSpec((k, 1), lambda i: (0, 0)),
+            pl.BlockSpec((1, length), lambda i: (0, 0)),
+        ],
+        out_specs=block,
+        out_shape=jax.ShapeDtypeStruct(received.shape, jnp.float32),
+        scratch_shapes=[pltpu.VMEM((chunk, k, length), jnp.float32)],
+    )(received, matrix, sq_s[:, None, None], sq_k[:, None], sq_l[None, :])
+
+
+def blocks(turned, parts):
+    first, length, last = turned.shape
+    turned = turned.reshape(first, parts, length // parts, last).transpose(1, 0, 2, 3)
+    return turned.reshape(parts, first, length // parts * last)
+
+
+def product_blocks(matrix, received, parts):
+    turned = jnp.dot(matrix, received.reshape(-1, received.shape[2]), precision=HIGH)
+    return turned.reshape(parts, turned.shape[0] // parts, turned.shape[1])
+
+
 def per_device(sizes, wave_coarse, potential_coarse, potential_fine):
     row, col = lax.axis_index("rows"), lax.axis_index("cols")
     rows, cols = sizes["rows"], sizes["cols"]
@@ -188,57 +292,59 @@
     partial_sum = jnp.sum(damped * damped)
 
     got, sums = exchange(
-        (give(damped, lift, cols), "cols"),
+        (blocks(jnp.einsum("xyz,zk->ykx", damped, lift, precision=HIGH), cols), "cols"),
         (jnp.full((cols, 8, 128), partial_sum, jnp.float32), "cols"),
     )
     partial_sum = jnp.sum(sums[:, 0, 0])
     got, sums = exchange(
-        (give(take(got, "cols", xr), lift, rows), "rows"),
+        (product_blocks(lift.T, got, rows), "rows"),
         (jnp.full((rows, 8, 128), partial_sum, jnp.float32), "rows"),
     )
     scale = lax.rsqrt(jnp.sum(sums[:, 0, 0]) / float(nc) ** 3 + EPSILON)
-    evolved = jnp.einsum("abl,lk->bak", take(got, "rows", xr), lift, precision=HIGH) * scale
+    evolved = assemble(got, nf // cols, lift) * scale
 
     density = evolved * evolved
-    near, far = fine_matrix[:, : nf // 2], fine_matrix[:, nf // 2 :]
-    swapped = density.transpose(1, 0, 2)
-    yr = nf // rows
+    half = nf // 2
+    near, far = fine_matrix[:, :half], fine_matrix[:, half:]
     got_near, got_far = exchange(
-        (give(swapped, near, rows), "rows"), (give(swapped, far, cols), "cols")
-    )
-    near_field, far_field = take(got_near, "rows", yr), take(got_far, "cols", yr)
-    near_rows = near_field.shape[0]
+        (blocks(jnp.einsum("zyx,xk->ykz", density, near, precision=HIGH), rows), "rows"),
+        (blocks(jnp.einsum("zyx,xk->zky", density, far, precision=HIGH), cols), "cols"),
+    )
     got_near, got_far = exchange(
-        (give(near_field, fine_matrix, cols), "cols"), (give(far_field, fine_matrix, rows), "rows")
-    )
-    near_field = apply(take(got_near, "cols", near_rows), fine_matrix)
-    far_field = apply(take(got_far, "rows", yr), fine_matrix)
+        (product_blocks(fine_matrix, got_near, cols), "cols"),
+        (product_blocks(fine_matrix, got_far, rows), "rows"),
+    )
     y_block, z_block = nf // cols, nf // rows
-    near_cols = nf // 2 // rows
-    far_cols = nf // 2 // cols
-    every = wavenumbers(nf, nf, 0, 1.0)[None, None, :] ** 2
-    near_field = near_field * dipolar_weights(
-        wavenumbers(nf, near_cols, row * near_cols, 1.0)[:, None, None] ** 2,
-        wavenumbers(nf, y_block, col * y_block, 1.0)[None, :, None] ** 2,
+    near_block, far_block = half // rows, half // cols
+    every = wavenumbers(nf, nf, 0, 1.0) ** 2
+    got_near = middle(
+        got_near,
+        fine_matrix,
+        wavenumbers(nf, near_block, row * near_block, 1.0) ** 2,
+        wavenumbers(nf, y_block, col * y_block, 1.0) ** 2,
         every,
-        nf,
-    )
-    far_field = far_field * dipolar_weights(
-        wavenumbers(nf, far_cols, nf // 2 + col * far_cols, 1.0)[None, :, None] ** 2,
+        2,
+    )
+    got_far = middle(
+        got_far,
+        fine_matrix,
+        wavenumbers(nf, far_block, half + col * far_block, 1.0) ** 2,
+        wavenumbers(nf, z_block, row * z_block, 1.0) ** 2,
         every,
-        wavenumbers(nf, z_block, row * z_block, 1.0)[:, None, None] ** 2,
-        nf,
-    )
+        1,
+    )
+    got_near, got_far = exchange((got_near, "cols"), (got_far, "rows"))
     got_near, got_far = exchange(
-        (give(near_field, fine_matrix, cols), "cols"), (give(far_field, fine_matrix, rows), "rows")
-    )
-    near_field, far_field = take(got_near, "cols", near_rows), take(got_far, "rows", z_block)
-    got_near, got_far = exchange(
-        (give(near_field, fine_matrix, rows), "rows"), (give(far_field, fine_matrix, cols), "cols")
-    )
-    near_field, far_field = take(got_near, "rows", near_rows), take(got_far, "cols", yr)
+        (product_blocks(fine_matrix, got_near, rows), "rows"),
+        (product_blocks(fine_matrix, got_far, cols), "cols"),
+    )
+    z_extent, y_extent = nf // cols, nf // rows
+    near_field = got_near.reshape(rows, y_extent, near_block, z_extent)
+    near_field = near_field.transpose(3, 1, 0, 2).reshape(z_extent, y_extent, half)
+    far_field = got_far.reshape(cols, z_extent, far_block, y_extent)
+    far_field = far_field.transpose(1, 3, 0, 2).reshape(z_extent, y_extent, half)
     spectrum = jnp.concatenate([near_field, far_field], axis=2)
-    field_dd = jnp.einsum("abl,lk->bak", spectrum, fine_matrix, precision=HIGH)
+    field_dd = jnp.einsum("zyk,kx->zyx", spectrum, fine_matrix, precision=HIGH)
     damped = jnp.exp(-TIME_STEP * (potential_fine + CONTACT * density + field_dd)) * evolved
     total = jnp.sum(damped * damped)
     for axis in ("rows", "cols"):

time: 1040 us -> 862 us (0.83)
  local copies, waits for them, and re-layouts: 314 us -> 128 us
  Pallas kernels: 550 us -> 592 us
  matrix products: 145 us -> 107 us
    reshape x24 -> x11, local copies, waits for them, and re-layouts: 109 us -> 22.9 us  [take(): received = received.reshape(parts, block, rows_extent, cols_extent)]
    dot_general x16 -> x6, matrix products: 77.6 us -> 10.1 us  [give(): turned = jnp.einsum('abl,lk->kab', values, matrix, precision=precision)]
    dot_general x2 -> x9, matrix products: 30 us -> 79.5 us  [the longest x5 38.9 us: product_blocks(): jnp.dot(matrix, received.reshape(-1, received.shape[2]), precision=HIGH)]
    reshape x16 -> x8, local copies, waits for them, and re-layouts: 61.7 us -> 16.8 us  [give(): return turned.reshape(parts, length // parts, rows_extent * cols_extent)]
    pallas_call x0 -> x3, Pallas kernels: none -> 41.7 us  [the longest x2 29.6 us: middle(): pl.pallas_call(functools.partial(middle_kernel, vertical, float(length) *...]
    dot_general x11 -> x3, local copies, waits for them, and re-layouts: 44.7 us -> 6.67 us  [give(): turned = jnp.einsum('abl,lk->kab', values, matrix, precision=precision)]
    reshape x2 -> x10, local copies, waits for them, and re-layouts: 14.6 us -> 52.3 us  [the longest x3 16 us: blocks(): return turned.reshape(parts, first, length // parts * last)]
    transpose x8 -> x4, local copies, waits for them, and re-layouts: 33 us -> 10.5 us  [take(): received.transpose(2, 1, 0, 3)]
where the time goes in v2:
time: 862 us; the launch traced here: 851 us
  Pallas kernels  592 us (69%)
  local copies, waits for them, and re-layouts  128 us (15%)
  matrix products  107 us (12%)
  other arithmetic  22.2 us (3%)
    pallas_call x14, Pallas kernels, __call__(): pl.pallas_call(functools.partial(exchange_kernel, axes, self.sizes), out_...  550 us
    dot_general x5, matrix products, product_blocks(): jnp.dot(matrix, received.reshape(-1, received.shape[2]), precision=HIGH)  38.9 us
    pallas_call x2, Pallas kernels, middle(): pl.pallas_call(functools.partial(middle_kernel, vertical, float(length) *...  29.6 us
    reshape x11, local copies, waits for them, and re-layouts, take(): received = received.reshape(parts, block, rows_extent, cols_extent)  22.9 us
    dot_general x1, matrix products, per_device(): field_dd = jnp.einsum('zyk,kx->zyx', spectrum, fine_matrix, precision=HIGH)  20.5 us

profile of v2, /device:TPU:0, one launch (start us, length us, event | category | flops | bytes accessed | tf_op | source)
XLA Modules:
  0.0 851.5 jit_solution(1493779955360760867)
XLA Ops:
  8.2 14.9 %exchange_0.1 = f32[4,48,1152]{2,1,0:T(8,128)} custom-call(f32[4,48,1152]{2,1,0:T(8,128)} %copy.110.refs_0_), custom_call_target="tpu_custom_call" | custom-call | tf_op jit(solution)/shard_map/exchange_0/pallas_call | solution.py:111
  31.0 19.7 %exchange_1.1 = f32[8,24,1152]{2,1,0:T(8,128)} custom-call(f32[8,24,1152]{2,1,0:T(8,128)} %fusion.155.refs_0_), custom_call_target="tpu_custom_call" | custom-call | tf_op jit(solution)/shard_map/exchange_1/pallas_call | solution.py:111
  65.7 23.1 %exchange_2.1 = (f32[4,48,1152]{2,1,0:T(8,128)}, f32[8,24,1152]{2,1,0:T(8,128)}) custom-call(f32[4,48,1152]{2,1,0:T(8,128)} %copy.112.refs_0_, f32[8,24,1152]{2,1,0:T(8,128)} %reshape.531.refs_1_), custom_call_target="tpu_custom_call" | custom-call | tf_op jit(solution)/shard_map/exchange_2/pallas_call | solution.py:111
  104.7 22.7 %exchange_3.1 = (f32[8,24,1152]{2,1,0:T(8,128)}, f32[4,48,1152]{2,1,0:T(8,128)}) custom-call(f32[8,24,1152]{2,1,0:T(8,128)} %fusion.156.refs_0_, f32[4,48,1152]{2,1,0:T(8,128)} %reshape.535.refs_1_), custom_call_target="tpu_custom_call" | custom-call | tf_op jit(solution)/shard_map/exchange_3/pallas_call | solution.py:111
  141.1 13.8 %exchange_4.1 = f32[4,48,1152]{2,1,0:T(8,128)} custom-call(f32[4,48,1152]{2,1,0:T(8,128)} %copy.113.refs_0_), custom_call_target="tpu_custom_call" | custom-call | tf_op jit(solution)/shard_map/exchange_4/pallas_call | solution.py:111
  162.8 21.6 %exchange_5.1 = f32[8,24,1152]{2,1,0:T(8,128)} custom-call(f32[8,24,1152]{2,1,0:T(8,128)} %fusion.157.refs_0_), custom_call_target="tpu_custom_call" | custom-call | tf_op jit(solution)/shard_map/exchange_5/pallas_call | solution.py:111
  219.6 23.4 %exchange_6.1 = (f32[4,48,2304]{2,1,0:T(8,128)}, f32[4,8,128]{2,1,0:T(8,128)}) custom-call(f32[4,48,2304]{2,1,0:T(8,128)} %copy.77.refs_0_, f32[4,8,128]{2,1,0:T(8,128)} %broadcast_in_dim.14.refs_1_), custom_call_target="tpu_custom_call" | custom-call | tf_op jit(solution)/shard_map/exchange_6/pallas_call | solution.py:111
  250.6 64.7 %exchange_7.1 = (f32[8,48,2304]{2,1,0:T(8,128)}, f32[8,8,128]{2,1,0:T(8,128)}) custom-call(f32[8,48,2304]{2,1,0:T(8,128)} %fusion.158.refs_0_, f32[8,8,128]{2,1,0:T(8,128)} %broadcast_in_dim.15.refs_1_), custom_call_target="tpu_custom_call" | custom-call | tf_op jit(solution)/shard_map/exchange_7/pallas_call | solution.py:111
  315.3 12.1 %shard_map.37 = f32[96,48,384]{2,1,0:T(8,128)} custom-call(f32[8,48,2304]{2,1,0:T(8,128)} %get-tuple-element.27.received, f32[192,384]{1,0:T(8,128)} %copy-done.6), custom_call_target="tpu_custom_call" | custom-call | tf_op jit(solution)/shard_map/pallas_call | solution.py:209
  335.7 8.9 %fusion.4 = f32[192,96,48]{1,0,2:T(8,128)S(1)} fusion(f32[96,48,384]{2,1,0:T(8,128)S(1)} %multiply_multiply_fusion, f32[384,384]{1,0:T(8,128)S(1)} %sine_add_fusion.matrix), kind=kOutput, calls=%fused_computation.6 | convolution fusion | flops 2038431744 | bytes 11010048 | tf_op jit(solution)/shard_map/zyx,xk->zky/dot_general | solution.py:311
  355.4 10.1 %fusion.6 = f32[192,96,48]{1,0,2:T(8,128)S(1)} fusion(f32[96,48,384]{2,1,0:T(8,128)} %copy-done.2, f32[384,384]{1,0:T(8,128)S(1)} %sine_add_fusion.matrix), kind=kOutput, calls=%fused_computation.8 | convolution fusion | flops 2038431744 | bytes 11010048 | tf_op jit(solution)/shard_map/zyx,xk->ykz/dot_general | solution.py:310
  373.2 79.1 %exchange_8.1 = (f32[8,48,2304]{2,1,0:T(8,128)}, f32[4,96,2304]{2,1,0:T(8,128)}) custom-call(f32[8,48,2304]{2,1,0:T(8,128)} %reshape.548.refs_0_, f32[4,96,2304]{2,1,0:T(8,128)} %copy.84.refs_1_), custom_call_target="tpu_custom_call" | custom-call | tf_op jit(solution)/shard_map/exchange_8/pallas_call | solution.py:111
  452.3 9.3 %fusion.32.refs_1_ = f32[8,48,2304]{2,1,0:T(8,128)} fusion(f32[384,2304,1]{1,0,2:T(8,128)} %bitcast.162, s32[8,48]{1,0:T(8,128)S(1)} %multiply_add_fusion), kind=kOutput, calls=%fused_computation.45 | convolution fusion | flops 2039906304 | bytes 7079424 | tf_op jit(solution)/shard_map/dot_general | solution.py:250
  461.6 7.7 fusion.28.refs_0_
  469.4 79.6 %exchange_9.1 = (f32[4,96,2304]{2,1,0:T(8,128)}, f32[8,48,2304]{2,1,0:T(8,128)}) custom-call(f32[4,96,2304]{2,1,0:T(8,128)} %fusion.28.refs_0_, f32[8,48,2304]{2,1,0:T(8,128)} %fusion.32.refs_1_), custom_call_target="tpu_custom_call" | custom-call | tf_op jit(solution)/shard_map/exchange_9/pallas_call | solution.py:111
  551.0 15.8 %shard_map.39.refs_1_ = f32[8,48,2304]{2,1,0:T(8,128)} custom-call(f32[8,48,2304]{2,1,0:T(8,128)} %get-tuple-element.32.received, f32[384,384]{1,0:T(8,128)} %copy-done.3, f32[48,1,1]{2,1,0:T(1,128)} %integer_pow.94.sq_s, f32[48,1]{1,0:T(8,128)} %integer_pow.95.sq_k, f32[1,384]{1,0:T(1,128)} %fusion.101.sq_l), custom_call_target="tpu_custom_call" | custom-call | tf_op jit(solution)/shard_map/pallas_call | solution.py:227
  568.3 13.7 %shard_map.38.refs_0_ = f32[4,96,2304]{2,1,0:T(8,128)} custom-call(f32[4,96,2304]{2,1,0:T(8,128)} %get-tuple-element.31.received, f32[384,384]{1,0:T(8,128)} %copy-done.3, f32[24,1,1]{2,1,0:T(1,128)} %integer_pow.91.sq_s, f32[96,1]{1,0:T(8,128)} %integer_pow.92.sq_k, f32[1,384]{1,0:T(1,128)} %fusion.101.sq_l), custom_call_target="tpu_custom_call" | custom-call | tf_op jit(solution)/shard_map/pallas_call | solution.py:227
  582.0 79.5 %exchange_10.1 = (f32[4,96,2304]{2,1,0:T(8,128)}, f32[8,48,2304]{2,1,0:T(8,128)}) custom-call(f32[4,96,2304]{2,1,0:T(8,128)} %shard_map.38.refs_0_, f32[8,48,2304]{2,1,0:T(8,128)} %shard_map.39.refs_1_), custom_call_target="tpu_custom_call" | custom-call | tf_op jit(solution)/shard_map/exchange_10/pallas_call | solution.py:111
  661.5 9.3 %fusion.26.refs_1_ = f32[4,96,2304]{2,1,0:T(8,128)} fusion(f32[384,2304,1]{1,0,2:T(8,128)} %bitcast.164, s32[4,96]{1,0:T(4,128)S(1)} %multiply_add_fusion.2), kind=kOutput, calls=%fused_computation.39 | convolution fusion | flops 2039906304 | bytes 7079424 | tf_op jit(solution)/shard_map/dot_general | solution.py:250
  670.9 7.7 fusion.30.refs_0_
  678.6 79.5 %exchange_11.1 = (f32[8,48,2304]{2,1,0:T(8,128)}, f32[4,96,2304]{2,1,0:T(8,128)}) custom-call(f32[8,48,2304]{2,1,0:T(8,128)} %fusion.30.refs_0_, f32[4,96,2304]{2,1,0:T(8,128)} %fusion.26.refs_1_), custom_call_target="tpu_custom_call" | custom-call | tf_op jit(solution)/shard_map/exchange_11/pallas_call | solution.py:111
  781.9 7.2 copy.101
  789.1 20.5 %multiply_reduce_fusion = (f32[]{:T(128)}, f32[96,48,384]{2,1,0:T(8,128)}) fusion(f32[96,48,192]{2,1,0:T(8,128)} %copy.101, f32[96,48,192]{2,1,0:T(8,128)} %copy.100, f32[96,48,384]{2,1,0:T(8,128)} %param.5, f32[96,48,384]{2,1,0:T(8,128)} %shard_map.37, f32[]{:T(128)S(6)} %rsqrt.6), kind=kOutput, calls=%fused_computation.4 | convolution fusion | flops 4096032768 | bytes 28311560 | tf_op jit(solution)/shard_map/zyk,kx->zyx/dot_general | solution.py:347
  811.0 23.8 %exchange_12.1 = f32[8,8,128]{2,1,0:T(8,128)} custom-call(f32[8,8,128]{2,1,0:T(8,128)} %broadcast_in_dim.16.refs_0_), custom_call_target="tpu_custom_call" | custom-call | tf_op jit(solution)/shard_map/exchange_12/pallas_call | solution.py:111
  (115 shorter events, 181.0 us)
Async XLA Ops:
  0.0 2.0 copy-start
  1.4 0.7 copy-start.7
  27.2 2.2 copy-start.8
  52.8 0.9 copy-start.9
  96.3 3.6 copy-start.10
  159.0 2.2 copy-start.11
  187.7 2.0 copy-start.12
  209.0 34.0 %copy-start.6 = (f32[192,384]{1,0:T(8,128)}, f32[192,384]{1,0:T(8,128)S(1)}, u32[]{:S(2)}) copy-start(f32[192,384]{1,0:T(8,128)S(1)} %fusion.64.matrix) | copy-start | bytes 884740
  333.2 11.4 %copy-start.2 = (f32[96,48,384]{2,1,0:T(8,128)}, f32[96,48,384]{2,1,0:T(8,128)S(1)}, u32[]{:S(2)}) copy-start(f32[96,48,384]{2,1,0:T(8,128)S(1)} %multiply_multiply_fusion) | copy-start | bytes 21233668
  335.6 19.8 %copy-start.3 = (f32[384,384]{1,0:T(8,128)}, f32[384,384]{1,0:T(8,128)S(1)}, u32[]{:S(2)}) copy-start(f32[384,384]{1,0:T(8,128)S(1)} %sine_add_fusion.matrix) | copy-start | bytes 1769476
  452.3 9.3 %copy-start.5 = (f32[8,48,2304]{2,1,0:T(8,128)S(1)}, f32[8,48,2304]{2,1,0:T(8,128)}, u32[]{:S(2)}) copy-start(f32[8,48,2304]{2,1,0:T(8,128)} %get-tuple-element.29) | copy-start | bytes 10616836
  661.5 9.3 %copy-start.4 = (f32[4,96,2304]{2,1,0:T(8,128)S(1)}, f32[4,96,2304]{2,1,0:T(8,128)}, u32[]{:S(2)}) copy-start(f32[4,96,2304]{2,1,0:T(8,128)} %get-tuple-element.33) | copy-start | bytes 10616836
  844.4 6.5 copy-start.1

commit v3 on v2

--- a/solution.py
+++ b/solution.py
@@ -179,22 +179,6 @@
     out[...] = product.reshape(out.shape)
 
 
-def middle_kernel(vertical, volume, received, matrix, sq_s, sq_k, sq_l, sent, held):
-    gather_pieces(received, held)
-    chunk, k, length = held.shape
-    values = split_product(held[...].reshape(chunk * k, length), matrix[...])
-    parts = [sq_s[...], sq_k[...][None], sq_l[...][None]]
-    parts = [jnp.broadcast_to(part, held.shape) for part in parts]
-    squares = parts[0] + parts[1] + parts[2]
-    nonzero = jnp.where(squares > 0, squares, 1.0)
-    weights = jnp.where(
-        squares > 0, DIPOLE_STRENGTH * (3.0 * parts[vertical] - squares) / nonzero, 0.0
-    )
-    values = values * (weights / volume).reshape(chunk * k, length)
-    held[...] = split_product(values, matrix[...]).reshape(held.shape)
-    scatter_pieces(held, sent)
-
-
 def chunk_of(spectators, width, k):
     for chunk in range(1, spectators):
         if spectators % chunk == 0 and chunk * width % 128 == 0 and chunk * k >= 256:
@@ -219,25 +203,163 @@
     )(received, matrix)
 
 
-def middle(received, matrix, sq_s, sq_k, sq_l, vertical):
-    parts, k, area = received.shape
-    spectators, length = sq_s.shape[0], matrix.shape[0]
-    chunk = chunk_of(spectators, area // spectators, k)
-    block = pl.BlockSpec((parts, k, area // spectators * chunk), lambda i: (0, 0, i))
+def halves(values):
+    high = values.astype(jnp.bfloat16)
+    return high, (values - high.astype(jnp.float32)).astype(jnp.bfloat16)
+
+
+def product_of(left, right):
+    product = functools.partial(jnp.dot, preferred_element_type=jnp.float32)
+    return product(left[0], right[0]) + (product(left[0], right[1]) + product(left[1], right[0]))
+
+
+def planes_kernel(flows, sizes, chunks, volume, *refs):
+    row, col = lax.axis_index("rows"), lax.axis_index("cols")
+
+    def place(axis, index):
+        return (index, col) if axis == "rows" else (row, index)
+
+    matrix = refs[0]
+    inputs = [refs[1 + 4 * i : 5 + 4 * i] for i in range(len(flows))]
+    at = 1 + 4 * len(flows)
+    outs = refs[at : at + len(flows)]
+    at += len(flows)
+    high, low = refs[at : at + 2]
+    at += 2
+    buffers = [refs[at + 9 * i : at + 9 * i + 9] for i in range(len(flows))]
+
+    barrier = pltpu.get_barrier_semaphore()
+    waits = 0
+    for axis in sorted(set(axis for axis, _ in flows)):
+        size = sizes[axis]
+        me = lax.axis_index(axis)
+        for step in range(1, size):
+            peer = lax.rem(me + step, size)
+            pl.semaphore_signal(barrier, inc=1, device_id=place(axis, peer), device_id_type=MESH)
+        waits += size - 1
+    high[...], low[...] = halves(matrix[...])
+    pl.semaphore_wait(barrier, waits)
+
+    def copies(flow, turn, c):
+        axis, _ = flows[flow]
+        size = sizes[axis]
+        me = lax.axis_index(axis)
+        sent, received = buffers[flow][2 * turn : 2 * turn + 2]
+        send_sem, recv_sem = buffers[flow][4 + 2 * turn : 6 + 2 * turn]
+        order = sorted(range(1, size), key=lambda step: abs(2 * step - size))
+        for step in order:
+            peer = lax.rem(me + step, size)
+            yield pltpu.make_async_remote_copy(
+                src_ref=sent.at[c, peer],
+                dst_ref=received.at[c, me],
+                send_sem=send_sem.at[c, step],
+                recv_sem=recv_sem.at[c, step],
+                device_id=place(axis, peer),
+                device_id_type=MESH,
+            )
+
+    def launch(flow, turn, c):
+        me = lax.axis_index(flows[flow][0])
+        for copy in copies(flow, turn, c):
+            copy.start()
+        sent, received = buffers[flow][2 * turn : 2 * turn + 2]
+        received[c, me] = sent[c, me]
+
+    def lanes(area, c):
+        if chunks == 1:
+            return slice(None)
+        return pl.ds(pl.multiple_of(c * (area // chunks), 128), area // chunks)
+
+    def first(c, carry):
+        for flow in range(len(flows)):
+            source, sent = inputs[flow][0], buffers[flow][0]
+            part = source[:, :, lanes(source.shape[2], c)]
+            part = part.reshape(matrix.shape[0], part.shape[2])
+            product = product_of((high[...], low[...]), halves(part))
+            sent[c] = product.reshape(sent.shape[1:])
+            launch(flow, 0, c)
+        return carry
+
+    def second(c, carry):
+        for flow in range(len(flows)):
+            _, sq_s, sq_k, sq_l = inputs[flow]
+            vertical = flows[flow][1]
+            held = buffers[flow][8]
+            chunk, k, length = held.shape
+            for copy in copies(flow, 0, c):
+                copy.wait_recv()
+            gather_pieces(buffers[flow][1].at[c], held)
+            both = (high[...], low[...])
+            values = product_of(halves(held[...].reshape(chunk * k, length)), both)
+            parts = [sq_s[pl.ds(c * chunk, chunk)], sq_k[...][None], sq_l[...][None]]
+            parts = [jnp.broadcast_to(part, held.shape) for part in parts]
+            squares = parts[0] + parts[1] + parts[2]
+            nonzero = jnp.where(squares > 0, squares, 1.0)
+            weights = jnp.where(
+                squares > 0, DIPOLE_STRENGTH * (3.0 * parts[vertical] - squares) / nonzero, 0.0
+            )
+            values = values * (weights / volume).reshape(chunk * k, length)
+            held[...] = product_of(halves(values), both).reshape(held.shape)
+            scatter_pieces(held, buffers[flow][2].at[c])
+            launch(flow, 1, c)
+        return carry
+
+    def third(c, carry):
+        for flow in range(len(flows)):
+            for copy in copies(flow, 1, c):
+                copy.wait_recv()
+            received, out = buffers[flow][3], outs[flow]
+            part = received[c].reshape(matrix.shape[0], received.shape[3])
+            product = product_of((high[...], low[...]), halves(part))
+            out[:, lanes(out.shape[1], c)] = product
+            for turn in range(2):
+                for copy in copies(flow, turn, c):
+                    copy.wait_send()
+        return carry
+
+    for stage in (first, second, third):
+        lax.fori_loop(0, chunks, stage, 0)
+
+
+def planes(exchange, flows, matrix):
+    sizes = exchange.sizes
+    length = matrix.shape[0]
+    counts = []
+    for axis, _, received, sq_s, sq_k, _ in flows:
+        spectators = sq_s.shape[0]
+        width = received.shape[2] // spectators
+        counts.append(spectators // chunk_of(spectators, width, sq_k.shape[0]))
+    chunks = counts[0] if len(set(counts)) == 1 else 1
+    operands, outs, scratch = [matrix], [], []
+    scratch += [pltpu.VMEM((length, length), jnp.bfloat16)] * 2
+    for axis, _, received, sq_s, sq_k, sq_l in flows:
+        operands += [received, sq_s[:, None, None], sq_k[:, None], sq_l[None, :]]
+        area, k, size = received.shape[2], sq_k.shape[0], sizes[axis]
+        outs.append(jax.ShapeDtypeStruct((length, area), jnp.float32))
+        scratch += [pltpu.VMEM((chunks, size, k, area // chunks), jnp.float32)] * 4
+        scratch += [pltpu.SemaphoreType.DMA((chunks, size))] * 4
+        scratch += [pltpu.VMEM((sq_s.shape[0] // chunks, k, length), jnp.float32)]
+    exchange.calls += 1
+    vmem = pl.BlockSpec(memory_space=pltpu.VMEM)
     return pl.pallas_call(
-        functools.partial(middle_kernel, vertical, float(length) ** 3),
-        grid=(spectators // chunk,),
-        in_specs=[
-            block,
-            pl.BlockSpec((length, length), lambda i: (0, 0)),
-            pl.BlockSpec((chunk, 1, 1), lambda i: (i, 0, 0)),
-            pl.BlockSpec((k, 1), lambda i: (0, 0)),
-            pl.BlockSpec((1, length), lambda i: (0, 0)),
-        ],
-        out_specs=block,
-        out_shape=jax.ShapeDtypeStruct(received.shape, jnp.float32),
-        scratch_shapes=[pltpu.VMEM((chunk, k, length), jnp.float32)],
-    )(received, matrix, sq_s[:, None, None], sq_k[:, None], sq_l[None, :])
+        functools.partial(
+            planes_kernel,
+            tuple((flow[0], flow[1]) for flow in flows),
+            sizes,
+            chunks,
+            float(length) ** 3,
+        ),
+        out_shape=outs,
+        in_specs=[vmem] * len(operands),
+        out_specs=[vmem] * len(outs),
+        scratch_shapes=scratch,
+        compiler_params=pltpu.CompilerParams(
+            collective_id=exchange.calls - 1,
+            has_side_effects=True,
+            vmem_limit_bytes=60 * 1024 * 1024,
+        ),
+        name=f"planes_{exchange.calls - 1}",
+    )(*operands)
 
 
 def blocks(turned, parts):
@@ -310,33 +432,29 @@
         (blocks(jnp.einsum("zyx,xk->ykz", density, near, precision=HIGH), rows), "rows"),
         (blocks(jnp.einsum("zyx,xk->zky", density, far, precision=HIGH), cols), "cols"),
     )
-    got_near, got_far = exchange(
-        (product_blocks(fine_matrix, got_near, cols), "cols"),
-        (product_blocks(fine_matrix, got_far, rows), "rows"),
-    )
     y_block, z_block = nf // cols, nf // rows
     near_block, far_block = half // rows, half // cols
     every = wavenumbers(nf, nf, 0, 1.0) ** 2
-    got_near = middle(
+    near_flow = (
+        "cols",
+        2,
         got_near,
-        fine_matrix,
         wavenumbers(nf, near_block, row * near_block, 1.0) ** 2,
         wavenumbers(nf, y_block, col * y_block, 1.0) ** 2,
         every,
-        2,
-    )
-    got_far = middle(
+    )
+    far_flow = (
+        "rows",
+        1,
         got_far,
-        fine_matrix,
         wavenumbers(nf, far_block, half + col * far_block, 1.0) ** 2,
         wavenumbers(nf, z_block, row * z_block, 1.0) ** 2,
         every,
-        1,
-    )
-    got_near, got_far = exchange((got_near, "cols"), (got_far, "rows"))
+    )
+    got_far, got_near = planes(exchange, (far_flow, near_flow), fine_matrix)
     got_near, got_far = exchange(
-        (product_blocks(fine_matrix, got_near, rows), "rows"),
-        (product_blocks(fine_matrix, got_far, cols), "cols"),
+        (got_near.reshape(rows, nf // rows, -1), "rows"),
+        (got_far.reshape(cols, nf // cols, -1), "cols"),
     )
     z_extent, y_extent = nf // cols, nf // rows
     near_field = got_near.reshape(rows, y_extent, near_block, z_extent)

time: 862 us -> 805 us (0.934)
  matrix products: 107 us -> 72.6 us
  Pallas kernels: 592 us -> 570 us
    pallas_call x14 -> x12, Pallas kernels: 550 us -> 377 us  [__call__(): pl.pallas_call(functools.partial(exchange_kernel, axes, self.sizes), out_...]
    pallas_call x2 -> x1, Pallas kernels: 29.6 us -> 181 us  [planes(): pl.pallas_call(functools.partial(planes_kernel, tuple(((flow[0], flow[1])...]
    dot_general x5 -> x1, matrix products: 38.9 us -> 4.85 us  [product_blocks(): jnp.dot(matrix, received.reshape(-1, received.shape[2]), precision=HIGH)]
where the time goes in v3:
time: 805 us; the launch traced here: 794 us
  Pallas kernels  570 us (71%)
  local copies, waits for them, and re-layouts  128 us (16%)
  matrix products  72.6 us (9%)
  other arithmetic  22.1 us (3%)
    pallas_call x12, Pallas kernels, __call__(): pl.pallas_call(functools.partial(exchange_kernel, axes, self.sizes), out_...  377 us
    pallas_call x1, Pallas kernels, planes(): pl.pallas_call(functools.partial(planes_kernel, tuple(((flow[0], flow[1])...  181 us
    reshape x11, local copies, waits for them, and re-layouts, take(): received = received.reshape(parts, block, rows_extent, cols_extent)  22.9 us
    dot_general x1, matrix products, per_device(): field_dd = jnp.einsum('zyk,kx->zyx', spectrum, fine_matrix, precision=HIGH)  20.5 us
    reshape x8, local copies, waits for them, and re-layouts, give(): return turned.reshape(parts, length // parts, rows_extent * cols_extent)  16.8 us

profile of v3, /device:TPU:0, one launch (start us, length us, event | category | flops | bytes accessed | tf_op | source)
XLA Modules:
  0.0 794.3 jit_solution(13635027741980080029)
XLA Ops:
  8.2 14.9 %exchange_0.1 = f32[4,48,1152]{2,1,0:T(8,128)} custom-call(f32[4,48,1152]{2,1,0:T(8,128)} %copy.110.refs_0_), custom_call_target="tpu_custom_call" | custom-call | tf_op jit(solution)/shard_map/exchange_0/pallas_call | solution.py:111
  31.0 19.7 %exchange_1.1 = f32[8,24,1152]{2,1,0:T(8,128)} custom-call(f32[8,24,1152]{2,1,0:T(8,128)} %fusion.109.refs_0_), custom_call_target="tpu_custom_call" | custom-call | tf_op jit(solution)/shard_map/exchange_1/pallas_call | solution.py:111
  65.7 23.1 %exchange_2.1 = (f32[4,48,1152]{2,1,0:T(8,128)}, f32[8,24,1152]{2,1,0:T(8,128)}) custom-call(f32[4,48,1152]{2,1,0:T(8,128)} %copy.112.refs_0_, f32[8,24,1152]{2,1,0:T(8,128)} %reshape.377.refs_1_), custom_call_target="tpu_custom_call" | custom-call | tf_op jit(solution)/shard_map/exchange_2/pallas_call | solution.py:111
  105.0 22.7 %exchange_3.1 = (f32[8,24,1152]{2,1,0:T(8,128)}, f32[4,48,1152]{2,1,0:T(8,128)}) custom-call(f32[8,24,1152]{2,1,0:T(8,128)} %fusion.110.refs_0_, f32[4,48,1152]{2,1,0:T(8,128)} %reshape.381.refs_1_), custom_call_target="tpu_custom_call" | custom-call | tf_op jit(solution)/shard_map/exchange_3/pallas_call | solution.py:111
  141.2 13.8 %exchange_4.1 = f32[4,48,1152]{2,1,0:T(8,128)} custom-call(f32[4,48,1152]{2,1,0:T(8,128)} %copy.113.refs_0_), custom_call_target="tpu_custom_call" | custom-call | tf_op jit(solution)/shard_map/exchange_4/pallas_call | solution.py:111
  162.9 21.6 %exchange_5.1 = f32[8,24,1152]{2,1,0:T(8,128)} custom-call(f32[8,24,1152]{2,1,0:T(8,128)} %fusion.111.refs_0_), custom_call_target="tpu_custom_call" | custom-call | tf_op jit(solution)/shard_map/exchange_5/pallas_call | solution.py:111
  200.0 6.4 multiply_reduce_fusion.1
  219.8 23.4 %exchange_6.1 = (f32[4,48,2304]{2,1,0:T(8,128)}, f32[4,8,128]{2,1,0:T(8,128)}) custom-call(f32[4,48,2304]{2,1,0:T(8,128)} %copy.77.refs_0_, f32[4,8,128]{2,1,0:T(8,128)} %broadcast_in_dim.14.refs_1_), custom_call_target="tpu_custom_call" | custom-call | tf_op jit(solution)/shard_map/exchange_6/pallas_call | solution.py:111
  250.7 64.7 %exchange_7.1 = (f32[8,48,2304]{2,1,0:T(8,128)}, f32[8,8,128]{2,1,0:T(8,128)}) custom-call(f32[8,48,2304]{2,1,0:T(8,128)} %fusion.112.refs_0_, f32[8,8,128]{2,1,0:T(8,128)} %broadcast_in_dim.15.refs_1_), custom_call_target="tpu_custom_call" | custom-call | tf_op jit(solution)/shard_map/exchange_7/pallas_call | solution.py:111
  315.4 12.1 %shard_map.37 = f32[96,48,384]{2,1,0:T(8,128)} custom-call(f32[8,48,2304]{2,1,0:T(8,128)} %get-tuple-element.25.received, f32[192,384]{1,0:T(8,128)} %copy-done.4), custom_call_target="tpu_custom_call" | custom-call | tf_op jit(solution)/shard_map/pallas_call | solution.py:193
  335.6 8.9 %fusion.4 = f32[192,96,48]{1,0,2:T(8,128)S(1)} fusion(f32[96,48,384]{2,1,0:T(8,128)S(1)} %multiply_multiply_fusion, f32[384,384]{1,0:T(8,128)S(1)} %sine_add_fusion.refs_0_), kind=kOutput, calls=%fused_computation.6 | convolution fusion | flops 2038431744 | bytes 11010048 | tf_op jit(solution)/shard_map/zyx,xk->zky/dot_general | solution.py:433
  349.6 5.6 copy.84.refs_1_
  355.3 10.1 %fusion.6 = f32[192,96,48]{1,0,2:T(8,128)S(1)} fusion(f32[96,48,384]{2,1,0:T(8,128)} %copy-done.2, f32[384,384]{1,0:T(8,128)S(1)} %sine_add_fusion.refs_0_), kind=kOutput, calls=%fused_computation.8 | convolution fusion | flops 2038431744 | bytes 11010048 | tf_op jit(solution)/shard_map/zyx,xk->ykz/dot_general | solution.py:432
  367.8 5.3 reshape.394.refs_0_
  373.1 79.1 %exchange_8.1 = (f32[8,48,2304]{2,1,0:T(8,128)}, f32[4,96,2304]{2,1,0:T(8,128)}) custom-call(f32[8,48,2304]{2,1,0:T(8,128)} %reshape.394.refs_0_, f32[4,96,2304]{2,1,0:T(8,128)} %copy.84.refs_1_), custom_call_target="tpu_custom_call" | custom-call | tf_op jit(solution)/shard_map/exchange_8/pallas_call | solution.py:111
  455.7 181.0 %planes_9.1 = (f32[384,2304]{1,0:T(8,128)}, f32[384,2304]{1,0:T(8,128)}) custom-call(f32[384,384]{1,0:T(8,128)} %copy-done.3, f32[4,96,2304]{2,1,0:T(8,128)} %get-tuple-element.27.refs_1_, f32[48,1,1]{2,1,0:T(1,128)} %integer_pow.91.refs_2_, f32[48,1]{1,0:T(8,128)} %integer_pow.92.refs_3_, f32[1,384]{1,0:T(1,128)} %fusion.67.refs_4_.refs_8_, ...), custom_call_target="tpu_custom_call" | custom-call | tf_op jit(solution)/shard_map/planes_9/pallas_call | solution.py:344
  636.7 64.7 %exchange_10.1 = (f32[8,48,2304]{2,1,0:T(8,128)}, f32[4,96,2304]{2,1,0:T(8,128)}) custom-call(f32[8,48,2304]{2,1,0:T(8,128)} %bitcast.138, f32[4,96,2304]{2,1,0:T(8,128)} %bitcast.137), custom_call_target="tpu_custom_call" | custom-call | tf_op jit(solution)/shard_map/exchange_10/pallas_call | solution.py:111
  701.4 6.2 reshape.399
  712.7 6.9 copy.100
  719.6 5.5 copy.98
  725.1 7.2 copy.101
  732.3 20.5 %multiply_reduce_fusion = (f32[]{:T(128)}, f32[96,48,384]{2,1,0:T(8,128)}) fusion(f32[96,48,192]{2,1,0:T(8,128)} %copy.101, f32[96,48,192]{2,1,0:T(8,128)} %copy.100, f32[96,48,384]{2,1,0:T(8,128)} %param.5, f32[96,48,384]{2,1,0:T(8,128)} %shard_map.37, f32[]{:T(128)S(6)} %rsqrt.6), kind=kOutput, calls=%fused_computation.4 | convolution fusion | flops 4096032768 | bytes 28311560 | tf_op jit(solution)/shard_map/zyk,kx->zyx/dot_general | solution.py:465
  753.9 23.8 %exchange_11.1 = f32[8,8,128]{2,1,0:T(8,128)} custom-call(f32[8,8,128]{2,1,0:T(8,128)} %broadcast_in_dim.16.refs_0_), custom_call_target="tpu_custom_call" | custom-call | tf_op jit(solution)/shard_map/exchange_11/pallas_call | solution.py:111
  787.4 6.5 broadcast_multiply_fusion
  (102 shorter events, 138.3 us)
Async XLA Ops:
  0.0 2.0 copy-start
  1.4 0.7 copy-start.5
  27.2 2.2 copy-start.6
  52.8 0.9 copy-start.7
  96.6 3.7 copy-start.8
  159.1 2.2 copy-start.9
  187.8 2.0 copy-start.10
  209.1 34.1 %copy-start.4 = (f32[192,384]{1,0:T(8,128)}, f32[192,384]{1,0:T(8,128)S(1)}, u32[]{:S(2)}) copy-start(f32[192,384]{1,0:T(8,128)S(1)} %fusion.30.matrix) | copy-start | bytes 884740
  333.2 11.4 %copy-start.2 = (f32[96,48,384]{2,1,0:T(8,128)}, f32[96,48,384]{2,1,0:T(8,128)S(1)}, u32[]{:S(2)}) copy-start(f32[96,48,384]{2,1,0:T(8,128)S(1)} %multiply_multiply_fusion) | copy-start | bytes 21233668
  335.6 19.7 %copy-start.3 = (f32[384,384]{1,0:T(8,128)}, f32[384,384]{1,0:T(8,128)S(1)}, u32[]{:S(2)}) copy-start(f32[384,384]{1,0:T(8,128)S(1)} %sine_add_fusion.refs_0_) | copy-start | bytes 1769476
  787.3 6.5 copy-start.1

commit v4 on v3

--- a/solution.py
+++ b/solution.py
@@ -190,6 +190,9 @@
     parts, k, area = received.shape
     chunk = chunk_of(spectators, area // spectators, k)
     length, points = matrix.shape
+    if k % 8:
+        held = received.reshape(parts, k, spectators, -1).transpose(2, 1, 0, 3)
+        return apply(held.reshape(spectators, k, length), matrix)
     return pl.pallas_call(
         assemble_kernel,
         grid=(spectators // chunk,),
@@ -385,30 +388,32 @@
     evolve = jnp.dot(coarse_matrix, decay * coarse_matrix, precision=HIGHEST)
     lift = jnp.dot(coarse_matrix, decay * lift_matrix(nc), precision=HIGHEST)
 
-    xr, yr, zr = nc // rows, nc // rows, nc // rows
-    (got,) = exchange((give(wave_coarse, evolve, cols), "cols"))
-    held = take(got, "cols", xr)
-    (got,) = exchange((give(held, evolve, rows), "rows"))
-    evolved = apply(take(got, "rows", xr), evolve)
+    xr = yr = nc // rows
+    spectators = nc // cols
+    turned = jnp.einsum("xyz,zk->ykx", wave_coarse, evolve, precision=HIGH)
+    (got,) = exchange((blocks(turned, cols), "cols"))
+    (got,) = exchange((product_blocks(evolve.T, got, rows), "rows"))
+    evolved = assemble(got, spectators, evolve)
+    turned = jnp.einsum("zyx,xk->zky", evolved * evolved, coarse_matrix, precision=HIGH)
     got, back = exchange(
-        (give(evolved * evolved, coarse_matrix, cols), "cols"), (give(evolved, None, rows), "rows")
-    )
-    held, back = take(got, "cols", yr), take(back, "rows", yr)
+        (blocks(turned, cols), "cols"), (give(evolved.transpose(1, 0, 2), None, rows), "rows")
+    )
+    back = take(back, "rows", yr)
     got, back = exchange(
-        (give(held, coarse_matrix, rows), "rows"), (give(back, None, cols), "cols")
-    )
-    spectrum, evolved = take(got, "rows", yr), take(back, "cols", xr)
+        (product_blocks(coarse_matrix, got, rows), "rows"), (give(back, None, cols), "cols")
+    )
+    spectrum, evolved = assemble(got, spectators, coarse_matrix), take(back, "cols", xr)
     z_block, x_block = nc // rows, nc // cols
     weights = dipolar_weights(
-        wavenumbers(nc, x_block, col * x_block, 2.0)[None, :, None] ** 2,
+        wavenumbers(nc, x_block, col * x_block, 2.0)[:, None, None] ** 2,
         wavenumbers(nc, nc, 0, 2.0)[None, None, :] ** 2,
-        wavenumbers(nc, z_block, row * z_block, 2.0)[:, None, None] ** 2,
+        wavenumbers(nc, z_block, row * z_block, 2.0)[None, :, None] ** 2,
         nc,
     )
-    spectrum = weights * apply(spectrum, coarse_matrix)
-    (got,) = exchange((give(spectrum, coarse_matrix, cols), "cols"))
-    (got,) = exchange((give(take(got, "cols", zr), coarse_matrix, rows), "rows"))
-    field_dd = apply(take(got, "rows", zr), coarse_matrix)
+    turned = jnp.einsum("xzy,yk->xkz", weights * spectrum, coarse_matrix, precision=HIGH)
+    (got,) = exchange((blocks(turned, cols), "cols"))
+    (got,) = exchange((product_blocks(coarse_matrix, got, rows), "rows"))
+    field_dd = assemble(got, spectators, coarse_matrix).transpose(1, 0, 2)
     density = evolved * evolved
     damped = jnp.exp(-TIME_STEP * (potential_coarse + CONTACT * density + field_dd)) * evolved
     partial_sum = jnp.sum(damped * damped)

time: 805 us -> 779 us (0.968)
  local copies, waits for them, and re-layouts: 128 us -> 89.5 us
  Pallas kernels: 570 us -> 583 us
  matrix products: 72.6 us -> 64.3 us
    dot_general x9 -> x3, matrix products: 23.3 us -> 5.09 us  [the longest x1 1.72 us: per_device(): jnp.einsum('zyx,xk->zky', evolved * evolved, coarse_matrix, precision=HIGH)]
    reshape x11 -> x3, local copies, waits for them, and re-layouts: 22.9 us -> 4.86 us  [take(): received = received.reshape(parts, block, rows_extent, cols_extent)]
    pallas_call x1 -> x4, Pallas kernels: 12.1 us -> 25.5 us  [assemble(): pl.pallas_call(assemble_kernel, grid=(spectators // chunk,), in_specs=[pl...]
    reshape x8 -> x2, local copies, waits for them, and re-layouts: 16.8 us -> 4.54 us  [give(): return turned.reshape(parts, length // parts, rows_extent * cols_extent)]
    transpose x5 -> x0, local copies, waits for them, and re-layouts: 11.8 us -> none  [the longest x4 10.5 us: take(): received.transpose(2, 1, 0, 3)]
    dot_general x1 -> x4, matrix products: 4.85 us -> 14.6 us  [product_blocks(): jnp.dot(matrix, received.reshape(-1, received.shape[2]), precision=HIGH)]
    reshape x3 -> x6, local copies, waits for them, and re-layouts: 15.9 us -> 20.9 us  [blocks(): return turned.reshape(parts, first, length // parts * last)]
where the time goes in v4:
time: 779 us; the launch traced here: 768 us
  Pallas kernels  583 us (75%)
  local copies, waits for them, and re-layouts  89.5 us (11%)
  matrix products  64.3 us (8%)
  other arithmetic  28.9 us (4%)
    pallas_call x12, Pallas kernels, __call__(): pl.pallas_call(functools.partial(exchange_kernel, axes, self.sizes), out_...  377 us
    pallas_call x1, Pallas kernels, planes(): pl.pallas_call(functools.partial(planes_kernel, tuple(((flow[0], flow[1])...  181 us
    pallas_call x4, Pallas kernels, assemble(): pl.pallas_call(assemble_kernel, grid=(spectators // chunk,), in_specs=[pl...  25.5 us
    reshape x6, local copies, waits for them, and re-layouts, blocks(): return turned.reshape(parts, first, length // parts * last)  20.9 us
    dot_general x1, matrix products, per_device(): field_dd = jnp.einsum('zyk,kx->zyx', spectrum, fine_matrix, precision=HIGH)  20.5 us
    reshape x6, local copies, waits for them, and re-layouts, blocks(): turned.reshape(first, parts, length // parts, last).transpose(1, 0, 2, 3)  15.6 us

profile of v4, /device:TPU:0, one launch (start us, length us, event | category | flops | bytes accessed | tf_op | source)
XLA Modules:
  0.0 767.9 jit_solution(1364449257972920656)
XLA Ops:
  7.6 14.9 %exchange_0.1 = f32[4,48,1152]{2,1,0:T(8,128)} custom-call(f32[4,48,1152]{2,1,0:T(8,128)} %copy.56.refs_0_), custom_call_target="tpu_custom_call" | custom-call | tf_op jit(solution)/shard_map/exchange_0/pallas_call | solution.py:111
  25.2 19.7 %exchange_1.1.received = f32[8,24,1152]{2,1,0:T(8,128)} custom-call(f32[8,24,1152]{2,1,0:T(8,128)} %fusion.118.refs_0_), custom_call_target="tpu_custom_call" | custom-call | tf_op jit(solution)/shard_map/exchange_1/pallas_call | solution.py:111
  59.4 23.1 %exchange_2.1 = (f32[4,48,1152]{2,1,0:T(8,128)}, f32[8,24,1152]{2,1,0:T(8,128)}) custom-call(f32[4,48,1152]{2,1,0:T(8,128)} %copy.61.refs_0_, f32[8,24,1152]{2,1,0:T(8,128)} %reshape.386.refs_1_), custom_call_target="tpu_custom_call" | custom-call | tf_op jit(solution)/shard_map/exchange_2/pallas_call | solution.py:111
  91.9 22.7 %exchange_3.1 = (f32[8,24,1152]{2,1,0:T(8,128)}, f32[4,48,1152]{2,1,0:T(8,128)}) custom-call(f32[8,24,1152]{2,1,0:T(8,128)} %fusion.51.refs_0_, f32[4,48,1152]{2,1,0:T(8,128)} %reshape.390.refs_1_), custom_call_target="tpu_custom_call" | custom-call | tf_op jit(solution)/shard_map/exchange_3/pallas_call | solution.py:111
  127.1 13.8 %exchange_4.1 = f32[4,48,1152]{2,1,0:T(8,128)} custom-call(f32[4,48,1152]{2,1,0:T(8,128)} %copy.67.refs_0_), custom_call_target="tpu_custom_call" | custom-call | tf_op jit(solution)/shard_map/exchange_4/pallas_call | solution.py:111
  144.5 21.6 %exchange_5.1.received = f32[8,24,1152]{2,1,0:T(8,128)} custom-call(f32[8,24,1152]{2,1,0:T(8,128)} %fusion.49.refs_0_), custom_call_target="tpu_custom_call" | custom-call | tf_op jit(solution)/shard_map/exchange_5/pallas_call | solution.py:111
  193.3 23.4 %exchange_6.1 = (f32[4,48,2304]{2,1,0:T(8,128)}, f32[4,8,128]{2,1,0:T(8,128)}) custom-call(f32[4,48,2304]{2,1,0:T(8,128)} %copy.70.refs_0_, f32[4,8,128]{2,1,0:T(8,128)} %broadcast_in_dim.14.refs_1_), custom_call_target="tpu_custom_call" | custom-call | tf_op jit(solution)/shard_map/exchange_6/pallas_call | solution.py:111
  224.3 64.7 %exchange_7.1 = (f32[8,48,2304]{2,1,0:T(8,128)}, f32[8,8,128]{2,1,0:T(8,128)}) custom-call(f32[8,48,2304]{2,1,0:T(8,128)} %fusion.119.refs_0_, f32[8,8,128]{2,1,0:T(8,128)} %broadcast_in_dim.15.refs_1_), custom_call_target="tpu_custom_call" | custom-call | tf_op jit(solution)/shard_map/exchange_7/pallas_call | solution.py:111
  289.0 12.1 %shard_map.40 = f32[96,48,384]{2,1,0:T(8,128)} custom-call(f32[8,48,2304]{2,1,0:T(8,128)} %get-tuple-element.25.received, f32[192,384]{1,0:T(8,128)} %copy-done.6), custom_call_target="tpu_custom_call" | custom-call | tf_op jit(solution)/shard_map/pallas_call | solution.py:196
  309.2 8.9 %fusion.4 = f32[192,96,48]{1,0,2:T(8,128)S(1)} fusion(f32[96,48,384]{2,1,0:T(8,128)S(1)} %multiply_multiply_fusion, f32[384,384]{1,0:T(8,128)S(1)} %sine_add_fusion.refs_0_), kind=kOutput, calls=%fused_computation.6 | convolution fusion | flops 2038431744 | bytes 11010048 | tf_op jit(solution)/shard_map/zyx,xk->zky/dot_general | solution.py:438
  318.1 5.1 copy.76
  323.2 5.6 copy.77.refs_1_
  328.9 10.1 %fusion.6 = f32[192,96,48]{1,0,2:T(8,128)S(1)} fusion(f32[96,48,384]{2,1,0:T(8,128)} %copy-done.2, f32[384,384]{1,0:T(8,128)S(1)} %sine_add_fusion.refs_0_), kind=kOutput, calls=%fused_computation.8 | convolution fusion | flops 2038431744 | bytes 11010048 | tf_op jit(solution)/shard_map/zyx,xk->ykz/dot_general | solution.py:437
  341.4 5.3 reshape.400.refs_0_
  346.7 79.1 %exchange_8.1 = (f32[8,48,2304]{2,1,0:T(8,128)}, f32[4,96,2304]{2,1,0:T(8,128)}) custom-call(f32[8,48,2304]{2,1,0:T(8,128)} %reshape.400.refs_0_, f32[4,96,2304]{2,1,0:T(8,128)} %copy.77.refs_1_), custom_call_target="tpu_custom_call" | custom-call | tf_op jit(solution)/shard_map/exchange_8/pallas_call | solution.py:111
  429.3 181.0 %planes_9.1 = (f32[384,2304]{1,0:T(8,128)}, f32[384,2304]{1,0:T(8,128)}) custom-call(f32[384,384]{1,0:T(8,128)} %copy-done.4, f32[4,96,2304]{2,1,0:T(8,128)} %get-tuple-element.27.refs_1_, f32[48,1,1]{2,1,0:T(1,128)} %integer_pow.91.refs_2_, f32[48,1]{1,0:T(8,128)} %integer_pow.92.refs_3_, f32[1,384]{1,0:T(1,128)} %fusion.75.refs_4_.refs_8_, ...), custom_call_target="tpu_custom_call" | custom-call | tf_op jit(solution)/shard_map/planes_9/pallas_call | solution.py:347
  610.3 64.7 %exchange_10.1 = (f32[8,48,2304]{2,1,0:T(8,128)}, f32[4,96,2304]{2,1,0:T(8,128)}) custom-call(f32[8,48,2304]{2,1,0:T(8,128)} %bitcast.137, f32[4,96,2304]{2,1,0:T(8,128)} %bitcast.136), custom_call_target="tpu_custom_call" | custom-call | tf_op jit(solution)/shard_map/exchange_10/pallas_call | solution.py:111
  675.0 6.2 reshape.405
  686.3 6.9 copy.93
  693.2 5.5 copy.91
  698.6 7.2 copy.94
  705.9 20.5 %multiply_reduce_fusion = (f32[]{:T(128)}, f32[96,48,384]{2,1,0:T(8,128)}) fusion(f32[96,48,192]{2,1,0:T(8,128)} %copy.94, f32[96,48,192]{2,1,0:T(8,128)} %copy.93, f32[96,48,384]{2,1,0:T(8,128)} %param.5, f32[96,48,384]{2,1,0:T(8,128)} %shard_map.40, f32[]{:T(128)S(6)} %rsqrt.6), kind=kOutput, calls=%fused_computation.4 | convolution fusion | flops 4096032768 | bytes 28311560 | tf_op jit(solution)/shard_map/zyk,kx->zyx/dot_general | solution.py:470
  727.5 23.8 %exchange_11.1 = f32[8,8,128]{2,1,0:T(8,128)} custom-call(f32[8,8,128]{2,1,0:T(8,128)} %broadcast_in_dim.16.refs_0_), custom_call_target="tpu_custom_call" | custom-call | tf_op jit(solution)/shard_map/exchange_11/pallas_call | solution.py:111
  760.9 6.5 broadcast_multiply_fusion
  (90 shorter events, 113.3 us)
Async XLA Ops:
  0.0 2.1 copy-start
  1.4 0.7 copy-start.7
  5.9 16.6 %copy-start.8 = (f32[192,192]{0,1:T(8,128)S(1)}, f32[192,192]{0,1:T(8,128)}, u32[]{:S(2)}) copy-start(f32[192,192]{0,1:T(8,128)} %copy-done.7) | copy-start | bytes 442372
  54.8 1.7 copy-start.3
  82.5 3.6 copy-start.10
  144.5 26.0 %copy-start.9 = (f32[4,48,1152]{2,1,0:T(8,128)S(1)}, f32[4,48,1152]{2,1,0:T(8,128)}, u32[]{:S(2)}) copy-start(f32[4,48,1152]{2,1,0:T(8,128)} %get-tuple-element.21) | copy-start | bytes 2654212
  174.4 2.8 copy-start.5
  182.5 34.2 %copy-start.6 = (f32[192,384]{1,0:T(8,128)}, f32[192,384]{1,0:T(8,128)S(1)}, u32[]{:S(2)}) copy-start(f32[192,384]{1,0:T(8,128)S(1)} %fusion.32.matrix) | copy-start | bytes 884740
  306.8 11.4 %copy-start.2 = (f32[96,48,384]{2,1,0:T(8,128)}, f32[96,48,384]{2,1,0:T(8,128)S(1)}, u32[]{:S(2)}) copy-start(f32[96,48,384]{2,1,0:T(8,128)S(1)} %multiply_multiply_fusion) | copy-start | bytes 21233668
  309.2 19.7 %copy-start.4 = (f32[384,384]{1,0:T(8,128)}, f32[384,384]{1,0:T(8,128)S(1)}, u32[]{:S(2)}) copy-start(f32[384,384]{1,0:T(8,128)S(1)} %sine_add_fusion.refs_0_) | copy-start | bytes 1769476
  760.9 6.5 copy-start.1
